TPU v7x, 32 devices: a whole 2x2x4 slice. The times are simulated.
32 devices in a mesh: grp: 4 (over x, core), seq: 8 (over z, y).
Axes of the slice: x: 2, y: 2, z: 4, core: 2. Of those that a mesh axis runs over, the one named last changes fastest.
Arguments:
- tokens: bfloat16 [32, 64, 128, 512], P(None, 'grp', 'seq'), may hold values from -6 to 6
- cotangent: bfloat16 [32, 64, 128, 512], P(None, 'grp', 'seq'), may hold values from -6 to 6
- gate_weight: bfloat16 [512, 512], replicated, may hold values from -0.25 to 0.25
- first_factor: bfloat16 [4, 32, 32], replicated, may hold values from -1 to 1
- middle_factor: bfloat16 [4, 64, 64], replicated, may hold values from -0.75 to 0.75
- last_factor: bfloat16 [4, 128, 128], replicated, may hold values from -0.5 to 0.5
Outputs:
- d_tokens: bfloat16 [32, 64, 128, 512], P(None, 'grp', 'seq')
- grad_gate: float32 [512, 512], P('seq')
- grad_first: float32 [4, 32, 32], replicated
- grad_middle: float32 [4, 64, 64], P(None, 'grp')
- grad_last: float32 [4, 128, 128], P(None, 'seq')
All inputs are finite; a program needn't handle non-finite values.
Results may differ from a plain program's by a relative error of at most 0.0065.
Values may be sent and summed in bfloat16 or wider, within the bound.
No kernel may reach another device: no remote copies, remote signals or barrier semaphores. Data moves between devices by JAX's collectives and lax.ppermute only.
A program may use at most 192 MiB of HBM per device.

v0:
```python
import math

import jax
import jax.numpy as jnp
from jax import lax
from jax.sharding import PartitionSpec as P

HEADS = 4


def headed(values):
    return values.reshape(values.shape[:-1] + (HEADS, values.shape[-1] // HEADS))


def mixing(weights, values, form):
    result = jnp.einsum(form, weights, headed(values), preferred_element_type=jnp.float32)
    return result.reshape(values.shape)


def contract(left, right, form):
    return jnp.einsum(form, headed(left), headed(right), preferred_element_type=jnp.float32)


def send_last(values):
    return lax.all_to_all(values, "seq", split_axis=0, concat_axis=2, tiled=True)


def send_middle(values):
    return lax.all_to_all(values, "grp", split_axis=2, concat_axis=1, tiled=True)


def return_middle(values):
    return lax.all_to_all(values, "grp", split_axis=1, concat_axis=2, tiled=True)


def return_last(values):
    return lax.all_to_all(values, "seq", split_axis=2, concat_axis=0, tiled=True)


def shards(tokens, cotangent, gate_weight, first_factor, middle_factor, last_factor):
    width = tokens.shape[-1]
    rows = tokens.reshape(-1, width)
    gate = jax.nn.sigmoid(jnp.dot(rows, gate_weight, preferred_element_type=jnp.float32)).reshape(
        tokens.shape
    )
    first_out = mixing(first_factor, tokens, "hab,bjkhe->ajkhe").astype(jnp.bfloat16)
    last_in = send_last(first_out)
    last_out = mixing(last_factor, last_in, "hab,ijbhe->ijahe").astype(jnp.bfloat16)
    middle_in = send_middle(last_out)
    middle_out = mixing(middle_factor, middle_in, "hab,ibkhe->iakhe").astype(jnp.bfloat16)
    mixer = return_last(return_middle(middle_out))
    upstream = cotangent.astype(jnp.float32)
    d_mix = (upstream * gate).astype(jnp.bfloat16)
    d_pre = (upstream * mixer.astype(jnp.float32) * gate * (1.0 - gate)).astype(jnp.bfloat16)
    pre_rows = d_pre.reshape(-1, width)
    gate_part = jnp.einsum("tc,td->cd", rows, pre_rows, preferred_element_type=jnp.float32)
    gate_term = jnp.einsum("td,cd->tc", pre_rows, gate_weight, preferred_element_type=jnp.float32)
    middle_grad_in = send_middle(send_last(d_mix))
    middle_back = mixing(middle_factor, middle_grad_in, "hba,ibkhe->iakhe").astype(jnp.bfloat16)
    middle_part = contract(middle_grad_in, middle_in, "iakhe,ibkhe->hab")
    last_back_in = return_middle(middle_back)
    last_back = mixing(last_factor, last_back_in, "hba,ijbhe->ijahe").astype(jnp.bfloat16)
    last_part = contract(last_back_in, last_in, "ijahe,ijbhe->hab")
    first_back_in = return_last(last_back)
    first_back = mixing(first_factor, first_back_in, "hba,bjkhe->ajkhe")
    first_part = contract(first_back_in, tokens, "ajkhe,bjkhe->hab")
    d_tokens = (
        (first_back.reshape(-1, width) + gate_term).astype(jnp.bfloat16).reshape(tokens.shape)
    )
    total = (
        tokens.shape[0]
        * tokens.shape[1]
        * tokens.shape[2]
        * lax.axis_size("grp")
        * lax.axis_size("seq")
    )
    factor = 1.0 / math.sqrt(total)
    gate_share, last_share = (
        lax.psum_scatter(gate_part, "seq", scatter_dimension=0, tiled=True),
        lax.psum_scatter(last_part, "seq", scatter_dimension=1, tiled=True),
    )
    middle_share = lax.psum_scatter(middle_part, "grp", scatter_dimension=1, tiled=True)
    gate_sum, last_sum, first_half = lax.psum((gate_share, last_share, first_part), "grp")
    middle_sum, first_sum = lax.psum((middle_share, first_half), "seq")
    return (d_tokens, gate_sum * factor, first_sum * factor, middle_sum * factor, last_sum * factor)


def solution(mesh):
    in_specs = (P(None, "grp", "seq", None), P(None, "grp", "seq", None), P(), P(), P(), P())
    out_specs = (
        P(None, "grp", "seq", None),
        P("seq", None),
        P(),
        P(None, "grp", None),
        P(None, "seq", None),
    )
    return jax.shard_map(shards, mesh=mesh, in_specs=in_specs, out_specs=out_specs, check_vma=False)
```

profile of v0, /device:TPU:0, one launch (start us, length us, event | category | flops | bytes accessed | tf_op | source)
XLA Modules:
  0.0 1805.6 jit_solution(3141081176804208275)
XLA Ops:
  19.7 15.6 convert_bitcast_fusion.3
  35.4 28.2 %copy.134 = bf16[32,16,16,4,128]{4,3,2,1,0:T(4,128)(2,1)} copy(bf16[32,16,16,4,128]{4,0,2,1,3:T(8,128)(2,1)S(1)} %convert_bitcast_fusion.3) | data formatting | bytes 16777216 | tf_op jit(solution)/shard_map/convert_element_type | solution.py:46
  63.6 13.1 convert_element_type.79
  76.7 190.4 %all_to_all.120 = bf16[32,16,16,512]{3,2,1,0:T(8,128)(2,1)} all-to-all(bf16[32,16,16,512]{3,2,1,0:T(8,128)(2,1)} %convert_element_type.79), channel_id=1, replica_groups=mesh['grp'=4,'seq'=8] {'seq'}, dimensions={0} | all-to-all | bytes 16777216 | tf_op jit(solution)/shard_map/all_to_all | solution.py:25
  275.2 12.6 reshape.71
  307.7 14.6 copy.138
  322.3 100.5 %all_to_all.121 = bf16[4,16,128,512]{3,1,0,2:T(8,128)(2,1)} all-to-all(bf16[4,16,128,512]{3,1,0,2:T(8,128)(2,1)} %copy.138), channel_id=1, replica_groups=mesh['grp'=4,'seq'=8] {'grp'}, dimensions={2} | all-to-all | bytes 16777216 | tf_op jit(solution)/shard_map/all_to_all | solution.py:29
  435.1 12.7 reshape.72
  447.9 14.9 convert_bitcast_fusion.1
  462.8 18.8 %copy.172 = bf16[4,64,32,4,128]{4,3,2,0,1:T(4,128)(2,1)} copy(bf16[4,64,32,4,128]{4,1,2,0,3:T(8,128)(2,1)S(1)} %convert_bitcast_fusion.1) | data formatting | bytes 16777216 | tf_op jit(solution)/shard_map/convert_element_type | solution.py:50
  481.6 13.1 reshape.87
  494.8 100.6 %all_to_all.122 = bf16[4,64,32,512]{3,2,0,1:T(8,128)(2,1)} all-to-all(bf16[4,64,32,512]{3,2,0,1:T(8,128)(2,1)} %reshape.87), channel_id=1, replica_groups=mesh['grp'=4,'seq'=8] {'grp'}, dimensions={1} | all-to-all | bytes 16777216 | tf_op jit(solution)/shard_map/all_to_all | solution.py:33
  631.7 171.3 %all-to-all-done.7 = bf16[4,16,128,512]{3,1,0,2:T(8,128)(2,1)} async-done(((bf16[4,16,128,512]{3,1,0,2:T(8,128)(2,1)}), bf16[4,16,128,512]{3,1,0,2:T(8,128)(2,1)}, u32[]{:S(2)}, u32[]{:S(2)}) %all-to-all-start.7) | async-done | bytes 8388640 | tf_op jit(solution)/shard_map/all_to_all | solution.py:37
  832.9 15.4 fusion.3
  848.3 188.7 %all_to_all.123 = bf16[32,16,16,512]{3,2,1,0:T(8,128)(2,1)} all-to-all(bf16[32,16,16,512]{3,2,1,0:T(8,128)(2,1)} %get-tuple-element.35), channel_id=1, replica_groups=mesh['grp'=4,'seq'=8] {'seq'}, dimensions={0} | all-to-all | bytes 16777216 | tf_op jit(solution)/shard_map/all_to_all | solution.py:25
  1056.5 100.5 %all_to_all.124 = bf16[4,16,128,512]{3,1,0,2:T(8,128)(2,1)} all-to-all(bf16[4,16,128,512]{3,1,0,2:T(8,128)(2,1)} %copy.118), channel_id=1, replica_groups=mesh['grp'=4,'seq'=8] {'grp'}, dimensions={2} | all-to-all | bytes 16777216 | tf_op jit(solution)/shard_map/all_to_all | solution.py:29
  1169.3 12.7 reshape.67
  1182.0 17.9 convert_bitcast_fusion.5
  1212.0 13.1 reshape.86
  1225.1 100.8 %all_to_all.125 = bf16[4,64,32,512]{3,2,0,1:T(8,128)(2,1)} all-to-all(bf16[4,64,32,512]{3,2,0,1:T(8,128)(2,1)} %reshape.86), channel_id=1, replica_groups=mesh['grp'=4,'seq'=8] {'grp'}, dimensions={1} | all-to-all | bytes 16777216 | tf_op jit(solution)/shard_map/all_to_all | solution.py:33
  1334.1 12.6 reshape.68
  1366.6 14.7 copy.127
  1397.2 189.2 %reduce-scatter.10.cloned.1.call-done = f32[64,512]{1,0:T(8,128)} async-done(((f32[512,512]{1,0:T(8,128)}), f32[64,512]{1,0:T(8,128)}) %reduce-scatter.10.cloned.1.call-update) | async-done | bytes 131088
  1588.2 31.5 %all-reduce.4.cloned.1.call-done = f32[64,512]{0,1:T(8,128)} async-done(((f32[64,512]{0,1:T(8,128)}), f32[64,512]{0,1:T(8,128)}) %all-reduce.4.cloned.1.call-update) | async-done | bytes 131088 | tf_op jit(solution)/shard_map/psum | solution.py:83
  1630.8 15.2 fusion.40
  1646.0 15.4 copy.129
  1661.4 12.6 reshape.69
  1674.0 20.3 %convolution_bitcast_fusion = f32[32,16,16,4,128]{4,0,2,1,3:T(8,128)} fusion(bf16[32,16,16,4,128]{4,3,2,1,0:T(4,128)(2,1)} %reshape.69, bf16[4,32,32]{2,1,0:T(8,128)(2,1)S(1)} %copy-done.5), kind=kOutput, calls=%fused_computation.10 | convolution fusion | flops 268435456 | bytes 25174016 | tf_op jit(solution)/shard_map/hba,bjkhe->ajkhe/dot_general | solution.py:16
  1694.3 14.7 fusion.45
  1720.7 38.9 %all-reduce = (f32[4,32,32]{2,1,0:T(8,128)S(1)}, f32[4,16,64]{2,1,0:T(8,128)S(1)}) all-reduce(f32[4,32,32]{2,1,0:T(8,128)S(1)} %get-tuple-element.32, f32[4,16,64]{2,1,0:T(8,128)} %reduce-scatter.6.cloned.1.call-done), channel_id=1, replica_groups=mesh['grp'=4,'seq'=8] {'seq'}, use_global_device_ids=true, to_apply=%region_3.0 | all-reduce | flops 8192 | bytes 65536 | tf_op jit(solution)/shard_map/psum | solution.py:84
  1761.5 21.1 %copy.132 = f32[32,16,16,4,128]{4,3,2,1,0:T(4,128)} copy(f32[32,16,16,4,128]{4,0,2,1,3:T(8,128)} %convolution_bitcast_fusion) | data formatting | bytes 33554432 | tf_op jit(solution)/shard_map/hba,bjkhe->ajkhe/transpose | solution.py:16
  1782.5 16.1 fusion.4
  (53 shorter events, 233.4 us)
Async XLA Ops:
  7.2 612.9 %copy-start = (bf16[512,512]{1,0:T(8,128)(2,1)S(1)}, bf16[512,512]{1,0:T(8,128)(2,1)}, u32[]{:S(2)}) copy-start(bf16[512,512]{1,0:T(8,128)(2,1)} %param.8) | copy-start | bytes 1572868
  7.2 12.6 copy-start.4
  275.2 12.6 copy-start.1
  435.1 12.7 copy-start.3
  614.9 188.1 %all-to-all-start.7 = ((bf16[4,16,128,512]{3,1,0,2:T(8,128)(2,1)}), bf16[4,16,128,512]{3,1,0,2:T(8,128)(2,1)}, u32[]{:S(2)}, u32[]{:S(2)}) async-start(bf16[4,16,128,512]{3,1,0,2:T(8,128)(2,1)} %copy.146), calls=%async_computation.7 | async-start | bytes 16777216 | tf_op jit(solution)/shard_map/all_to_all | solution.py:37
  1334.1 12.6 copy-start.2
  1381.2 264.8 %all-to-all-start.3 = ((bf16[4,16,128,512]{3,1,0,2:T(8,128)(2,1)}), bf16[4,16,128,512]{3,1,0,2:T(8,128)(2,1)}, u32[]{:S(2)}, u32[]{:S(2)}) async-start(bf16[4,16,128,512]{3,1,0,2:T(8,128)(2,1)} %copy.127), calls=%async_computation.3 | async-start | bytes 16777216 | tf_op jit(solution)/shard_map/all_to_all | solution.py:37
  1386.3 200.1 %reduce-scatter.10.cloned.1.call-start = ((), (), s32[]{:S(2)}) async-start(), calls=%async_computation.14 | async-start | bytes 1179648
  1397.2 222.6 %all-reduce.4.cloned.1.call-start = ((), (), s32[]{:S(2)}) async-start(), calls=%async_computation.11 | async-start | bytes 524288 | tf_op jit(solution)/shard_map/psum | solution.py:83
  1588.2 120.9 %reduce-scatter.8.cloned.1.call-start = ((), (), s32[]{:S(2)}) async-start(), calls=%async_computation.13 | async-start | bytes 294912 | tf_op jit(solution)/shard_map/reduce_scatter | solution.py:80
  1630.3 90.4 %reduce-scatter.6.cloned.1.call-start = ((), (), s32[]{:S(2)}) async-start(), calls=%async_computation.12 | async-start | bytes 163840 | tf_op jit(solution)/shard_map/reduce_scatter | solution.py:82
  1661.4 12.6 copy-start.5
Sparse Core Ops, SparseCore 0:
  1397.3 189.0 reduce-scatter.9
  1588.7 30.9 all-reduce.3
  1630.4 62.5 reduce-scatter.7
  1695.2 18.7 reduce-scatter.5
where the time goes:
time: 1820 us; the launch traced here: 1810 us
  blocking collectives  832 us (46%)
  waiting for transfers between devices  392 us (22%)
  local copies, waits for them, and re-layouts  363 us (20%)
  matrix products  164 us (9%)
  other arithmetic  29.7 us (2%)
    all_to_all x2, blocking collectives, send_last(): lax.all_to_all(values, 'seq', split_axis=0, concat_axis=2, tiled=True)  379 us
    all_to_all x2, blocking collectives, return_middle(): lax.all_to_all(values, 'grp', split_axis=1, concat_axis=2, tiled=True)  201 us
    all_to_all x2, blocking collectives, send_middle(): lax.all_to_all(values, 'grp', split_axis=2, concat_axis=1, tiled=True)  201 us
    unnamed x5, waiting for transfers between devices  189 us
    all_to_all x2, waiting for transfers between devices, return_last(): lax.all_to_all(values, 'seq', split_axis=2, concat_axis=0, tiled=True)  171 us
    dot_general x6, matrix products, mixing(): jnp.einsum(form, weights, headed(values), preferred_element_type=jnp.floa...  87.8 us
    reshape x6, local copies, waits for them, and re-layouts, headed(): values.reshape(values.shape[:-1] + (HEADS, values.shape[-1] // HEADS))  75.7 us
    convert_element_type x2, local copies, waits for them, and re-layouts, shards(): mixing(first_factor, tokens, 'hab,bjkhe->ajkhe').astype(jnp.bfloat16)  41.3 us
  transfers between devices with their start and end apart: 6, of which 3 were waited for; matrix products, arithmetic and copies ran while one was open for 6% of the time, Pallas kernels for 0%

commit v1 on v0

v1 whole, which is shorter than its diff:
```python
import functools
import math

import jax
import jax.numpy as jnp
from jax import lax
from jax.experimental import pallas as pl
from jax.experimental.pallas import tpu as pltpu
from jax.sharding import PartitionSpec as P

HEADS = 4
ALL = ("grp", "seq")
F32 = jnp.float32
BF16 = jnp.bfloat16


def headed(values):
    return values.reshape(values.shape[:-1] + (HEADS, values.shape[-1] // HEADS))


def mixing(weights, values, form):
    result = jnp.einsum(form, weights, headed(values), preferred_element_type=F32)
    return result.reshape(values.shape)


def contract(left, right, form):
    return jnp.einsum(form, headed(left), headed(right), preferred_element_type=F32)


def send_last(values):
    return lax.all_to_all(values, "seq", split_axis=0, concat_axis=2, tiled=True)


def send_middle(values):
    return lax.all_to_all(values, "grp", split_axis=2, concat_axis=1, tiled=True)


def return_middle(values):
    return lax.all_to_all(values, "grp", split_axis=1, concat_axis=2, tiled=True)


def return_last(values):
    return lax.all_to_all(values, "seq", split_axis=2, concat_axis=0, tiled=True)


def positions(tokens):
    return math.prod(tokens.shape[:3]) * lax.axis_size("grp") * lax.axis_size("seq")


def general(tokens, cotangent, gate_weight, first_factor, middle_factor, last_factor):
    width = tokens.shape[-1]
    rows = tokens.reshape(-1, width)
    gate = jax.nn.sigmoid(jnp.dot(rows, gate_weight, preferred_element_type=F32))
    gate = gate.reshape(tokens.shape)
    first_out = mixing(first_factor, tokens, "hab,bjkhe->ajkhe").astype(BF16)
    last_in = send_last(first_out)
    last_out = mixing(last_factor, last_in, "hab,ijbhe->ijahe").astype(BF16)
    middle_in = send_middle(last_out)
    middle_out = mixing(middle_factor, middle_in, "hab,ibkhe->iakhe").astype(BF16)
    mixer = return_last(return_middle(middle_out))
    upstream = cotangent.astype(F32)
    d_mix = (upstream * gate).astype(BF16)
    d_pre = (upstream * mixer.astype(F32) * gate * (1.0 - gate)).astype(BF16)
    pre_rows = d_pre.reshape(-1, width)
    gate_part = jnp.einsum("tc,td->cd", rows, pre_rows, preferred_element_type=F32)
    gate_term = jnp.einsum("td,cd->tc", pre_rows, gate_weight, preferred_element_type=F32)
    middle_grad_in = send_middle(send_last(d_mix))
    middle_back = mixing(middle_factor, middle_grad_in, "hba,ibkhe->iakhe").astype(BF16)
    middle_part = contract(middle_grad_in, middle_in, "iakhe,ibkhe->hab")
    last_back_in = return_middle(middle_back)
    last_back = mixing(last_factor, last_back_in, "hba,ijbhe->ijahe").astype(BF16)
    last_part = contract(last_back_in, last_in, "ijahe,ijbhe->hab")
    first_back_in = return_last(last_back)
    first_back = mixing(first_factor, first_back_in, "hba,bjkhe->ajkhe")
    first_part = contract(first_back_in, tokens, "ajkhe,bjkhe->hab")
    d_tokens = (first_back.reshape(-1, width) + gate_term).astype(BF16).reshape(tokens.shape)
    return (d_tokens,) + reduced(
        gate_part, first_part, middle_part, last_part, 1.0 / math.sqrt(positions(tokens))
    )


def reduced(gate_part, first_part, middle_part, last_part, factor):
    gate_share = lax.psum_scatter(gate_part, "seq", scatter_dimension=0, tiled=True)
    last_share = lax.psum_scatter(last_part, "seq", scatter_dimension=1, tiled=True)
    middle_share = lax.psum_scatter(middle_part, "grp", scatter_dimension=1, tiled=True)
    gate_sum, last_sum, first_half = lax.psum((gate_share, last_share, first_part), "grp")
    middle_sum, first_sum = lax.psum((middle_share, first_half), "seq")
    return gate_sum * factor, first_sum * factor, middle_sum * factor, last_sum * factor


def exchange(values):
    return lax.all_to_all(values, ALL, split_axis=0, concat_axis=0, tiled=True)


def dot(left, right):
    return jnp.dot(left, right, preferred_element_type=F32)


def dot_rows(left, right):
    return lax.dot_general(left, right, (((1,), (1,)), ((), ())), preferred_element_type=F32)


def spread(factor, lanes, turned=False):
    size = factor.shape[0]
    wide = size * lanes
    rows = lax.broadcasted_iota(jnp.int32, (wide, size), 0) // lanes
    tall = jnp.where(rows == lax.broadcasted_iota(jnp.int32, (wide, size), 1), 1.0, 0.0).astype(BF16)
    columns = lax.broadcasted_iota(jnp.int32, (size, wide), 1) // lanes
    flat = jnp.where(columns == lax.broadcasted_iota(jnp.int32, (size, wide), 0), 1.0, 0.0).astype(BF16)
    picked = (dot_rows if turned else dot)(tall, factor).astype(BF16)
    row = lax.broadcasted_iota(jnp.int32, (wide, wide), 0) % lanes
    column = lax.broadcasted_iota(jnp.int32, (wide, wide), 1) % lanes
    return jnp.where(row == column, dot(picked, flat), 0.0).astype(BF16)


def gather_diagonal(total, size, lanes):
    wide = size * lanes
    row = lax.broadcasted_iota(jnp.int32, (wide, wide), 0) % lanes
    column = lax.broadcasted_iota(jnp.int32, (wide, wide), 1) % lanes
    kept = jnp.where(row == column, total, 0.0).reshape(size, lanes, wide).sum(axis=1)
    owner = lax.broadcasted_iota(jnp.int32, (wide, size), 0) // lanes
    target = lax.broadcasted_iota(jnp.int32, (wide, size), 1)
    collect = jnp.where(owner == target, 1.0, 0.0)
    return jnp.dot(kept, collect, precision=lax.Precision.HIGHEST, preferred_element_type=F32)


def gate_of(rows, weight):
    return jax.nn.sigmoid(dot(rows, weight))


def open_kernel(n_i, step_j, lanes, width, x_ref, g_ref, w_ref, a_ref, v_ref, wide):
    size = width // HEADS

    @pl.when(pl.program_id(0) == 0)
    def _():
        for h in range(HEADS):
            wide[h] = spread(a_ref[h], lanes, turned=True)

    sent = []
    for j in range(step_j):
        rows = x_ref[:, j].reshape(n_i * lanes, width)
        up = g_ref[:, j].reshape(n_i * lanes, width).astype(F32)
        sent.append((up * gate_of(rows, w_ref[...])).astype(BF16))
    for h in range(HEADS):
        pair = jnp.concatenate([d[:, h * size : (h + 1) * size] for d in sent], axis=1)
        out = dot(wide[h], pair).astype(BF16)
        for j in range(step_j):
            v_ref[:, j, :, h * size : (h + 1) * size] = out[:, j * size : (j + 1) * size].reshape(
                n_i, lanes, size
            )


def open_side(tokens, cotangent, gate_weight, first_factor):
    n_i, n_j, lanes, width = tokens.shape
    step_j = 2
    block = pl.BlockSpec((n_i, step_j, lanes, width), lambda j: (0, j, 0, 0))
    whole = lambda a: pl.BlockSpec(a.shape, lambda j: (0,) * a.ndim)
    count = tokens.size
    return pl.pallas_call(
        functools.partial(open_kernel, n_i, step_j, lanes, width),
        grid=(n_j // step_j,),
        in_specs=[block, block, whole(gate_weight), whole(first_factor)],
        out_specs=block,
        out_shape=jax.ShapeDtypeStruct(tokens.shape, BF16),
        scratch_shapes=[pltpu.VMEM((HEADS, n_i * lanes, n_i * lanes), BF16)],
        cost_estimate=pl.CostEstimate(
            flops=2 * count * (width + n_i * lanes), bytes_accessed=6 * count, transcendentals=count
        ),
        name="open_side",
    )(tokens, cotangent, gate_weight, first_factor)


def forward_kernel(groups, blocks, n_j, lanes, size, x_ref, b_ref, c_ref, bx_ref, y_ref, wide):
    last = b_ref[0]
    wide[...] = spread(c_ref[0], lanes)

    def over_last(t, carry):
        g, j = t // (n_j // 2), (t % (n_j // 2)) * 2
        pair = [x_ref[g, :, j + p].reshape(blocks * lanes, size) for p in range(2)]
        out = dot(last, jnp.concatenate(pair, axis=1)).astype(BF16)
        for p in range(2):
            bx_ref[g, :, j + p] = out[:, p * size : (p + 1) * size].reshape(blocks, lanes, size)
        return carry

    lax.fori_loop(0, groups * n_j // 2, over_last, 0, unroll=2)

    def over_middle(t, carry):
        pair = [bx_ref[:, 2 * t + p].reshape(groups * n_j * lanes, size) for p in range(2)]
        out = dot(wide[...], jnp.concatenate(pair, axis=1)).astype(BF16)
        for p in range(2):
            y_ref[:, 2 * t + p] = out[:, p * size : (p + 1) * size].reshape(groups, n_j, lanes, size)
        return carry

    lax.fori_loop(0, blocks // 2, over_middle, 0)


def forward_side(values, last_factor, middle_factor):
    groups, blocks, n_j, lanes, width = values.shape
    size = width // HEADS
    block = pl.BlockSpec((groups, blocks, n_j, lanes, size), lambda h: (0, 0, 0, 0, h))
    one = lambda a: pl.BlockSpec((1,) + a.shape[1:], lambda h: (h, 0, 0))
    count = values.size
    return pl.pallas_call(
        functools.partial(forward_kernel, groups, blocks, n_j, lanes, size),
        grid=(HEADS,),
        in_specs=[block, one(last_factor), one(middle_factor)],
        out_specs=[block, block],
        out_shape=[jax.ShapeDtypeStruct(values.shape, BF16)] * 2,
        scratch_shapes=[pltpu.VMEM((groups * n_j * lanes, groups * n_j * lanes), BF16)],
        cost_estimate=pl.CostEstimate(
            flops=2 * count * (middle_factor.shape[1] * lanes + last_factor.shape[1]),
            bytes_accessed=6 * count,
            transcendentals=0,
        ),
        name="forward_side",
    )(values, last_factor, middle_factor)


def backward_kernel(
    groups, blocks, n_j, lanes, size, v_ref, x_ref, bx_ref, b_ref, c_ref, u_ref, gl_ref, gm_ref, cv, acc, wide
):
    rows = groups * n_j * lanes
    wide[...] = spread(c_ref[0], lanes, turned=True)
    acc[...] = jnp.zeros_like(acc)

    def over_middle(t, carry):
        pair = [v_ref[:, 2 * t + p].reshape(rows, size) for p in range(2)]
        sent = jnp.concatenate(pair, axis=1)
        held = [bx_ref[:, 2 * t + p].reshape(rows, size) for p in range(2)]
        acc[...] += dot_rows(sent, jnp.concatenate(held, axis=1))
        out = dot(wide[...], sent).astype(BF16)
        for p in range(2):
            cv[:, 2 * t + p] = out[:, p * size : (p + 1) * size].reshape(groups, n_j, lanes, size)
        return carry

    lax.fori_loop(0, blocks // 2, over_middle, 0)
    gm_ref[0] = gather_diagonal(acc[...], groups * n_j, lanes)
    last = b_ref[0]

    def over_last(t, total):
        g, j = t // (n_j // 2), (t % (n_j // 2)) * 2
        pair = [cv[g, :, j + p].reshape(blocks * lanes, size) for p in range(2)]
        back = jnp.concatenate(pair, axis=1)
        held = [x_ref[g, :, j + p].reshape(blocks * lanes, size) for p in range(2)]
        out = dot(last, back).astype(BF16)
        for p in range(2):
            u_ref[g, :, j + p] = out[:, p * size : (p + 1) * size].reshape(blocks, lanes, size)
        return total + dot_rows(back, jnp.concatenate(held, axis=1))

    zero = jnp.zeros((blocks * lanes, blocks * lanes), F32)
    gl_ref[0] = lax.fori_loop(0, groups * n_j // 2, over_last, zero, unroll=2)


def backward_side(sent, values, mixed, last_factor_t, middle_factor):
    groups, blocks, n_j, lanes, width = values.shape
    size = width // HEADS
    n_middle, n_last = groups * n_j, blocks * lanes
    block = pl.BlockSpec((groups, blocks, n_j, lanes, size), lambda h: (0, 0, 0, 0, h))
    one = lambda *shape: pl.BlockSpec((1,) + shape, lambda h: (h, 0, 0))
    count = values.size
    return pl.pallas_call(
        functools.partial(backward_kernel, groups, blocks, n_j, lanes, size),
        grid=(HEADS,),
        in_specs=[block] * 3 + [one(n_last, n_last), one(n_middle, n_middle)],
        out_specs=[block, one(n_last, n_last), one(n_middle, n_middle)],
        out_shape=[
            jax.ShapeDtypeStruct(values.shape, BF16),
            jax.ShapeDtypeStruct((HEADS, n_last, n_last), F32),
            jax.ShapeDtypeStruct((HEADS, n_middle, n_middle), F32),
        ],
        scratch_shapes=[
            pltpu.VMEM((groups, blocks, n_j, lanes, size), BF16),
            pltpu.VMEM((n_middle * lanes, n_middle * lanes), F32),
            pltpu.VMEM((n_middle * lanes, n_middle * lanes), BF16),
        ],
        cost_estimate=pl.CostEstimate(
            flops=4 * count * (n_middle * lanes + n_last), bytes_accessed=8 * count, transcendentals=0
        ),
        name="backward_side",
    )(sent, values, mixed, last_factor_t, middle_factor)


def close_kernel(
    n_i, step_j, lanes, width, x_ref, g_ref, y_ref, w_ref, a_ref, t_ref, gg_ref, gf_ref, acc, wide
):
    size = width // HEADS
    rows_n = n_i * lanes

    @pl.when(pl.program_id(0) == 0)
    def _():
        acc[...] = jnp.zeros_like(acc)
        gg_ref[...] = jnp.zeros_like(gg_ref)
        for h in range(HEADS):
            wide[h] = spread(a_ref[h], lanes)

    rows, ups, gates, mixes, sent = [], [], [], [], []
    for j in range(step_j):
        rows.append(x_ref[:, j].reshape(rows_n, width))
        ups.append(g_ref[:, j].reshape(rows_n, width).astype(F32))
        gates.append(gate_of(rows[j], w_ref[...]))
        mixes.append(y_ref[:, j].reshape(rows_n, width))
        sent.append((ups[j] * gates[j]).astype(BF16))
    outs = []
    for h in range(HEADS):
        cut = slice(h * size, (h + 1) * size)
        held = jnp.concatenate([m[:, cut] for m in mixes], axis=1)
        back = jnp.concatenate([d[:, cut] for d in sent], axis=1)
        acc[h] += dot_rows(back, held)
        outs.append(dot(wide[h], held).astype(BF16).astype(F32))
    for j in range(step_j):
        mixer = jnp.concatenate([o[:, j * size : (j + 1) * size] for o in outs], axis=1)
        d_pre = (ups[j] * mixer * gates[j] * (1.0 - gates[j])).astype(BF16)
        t_ref[:, j] = dot_rows(d_pre, w_ref[...]).astype(BF16).reshape(n_i, lanes, width)
        gg_ref[...] += lax.dot_general(
            rows[j], d_pre, (((0,), (0,)), ((), ())), preferred_element_type=F32
        )

    @pl.when(pl.program_id(0) == pl.num_programs(0) - 1)
    def _():
        for h in range(HEADS):
            gf_ref[h] = gather_diagonal(acc[h], n_i, lanes)


def close_side(tokens, cotangent, mixed, gate_weight, first_factor):
    n_i, n_j, lanes, width = tokens.shape
    step_j = 2
    block = pl.BlockSpec((n_i, step_j, lanes, width), lambda j: (0, j, 0, 0))
    whole = lambda shape: pl.BlockSpec(shape, lambda j: (0,) * len(shape))
    count = tokens.size
    return pl.pallas_call(
        functools.partial(close_kernel, n_i, step_j, lanes, width),
        grid=(n_j // step_j,),
        in_specs=[block, block, block, whole(gate_weight.shape), whole(first_factor.shape)],
        out_specs=[block, whole((width, width)), whole((HEADS, n_i, n_i))],
        out_shape=[
            jax.ShapeDtypeStruct(tokens.shape, BF16),
            jax.ShapeDtypeStruct((width, width), F32),
            jax.ShapeDtypeStruct((HEADS, n_i, n_i), F32),
        ],
        scratch_shapes=[
            pltpu.VMEM((HEADS, n_i * lanes, n_i * lanes), F32),
            pltpu.VMEM((HEADS, n_i * lanes, n_i * lanes), BF16),
        ],
        cost_estimate=pl.CostEstimate(
            flops=2 * count * (3 * width + 2 * n_i * lanes),
            bytes_accessed=8 * count,
            transcendentals=count,
        ),
        name="close_side",
    )(tokens, cotangent, mixed, gate_weight, first_factor)


def direct(tokens, cotangent, gate_weight, first_factor, middle_factor, last_factor):
    groups, blocks = lax.axis_size("grp"), lax.axis_size("seq")
    split = (groups, blocks) + tokens.shape[1:]
    at_whole = exchange(tokens).reshape(split)
    sent = open_side(tokens, cotangent, gate_weight, first_factor)
    sent_whole = exchange(sent).reshape(split)
    mixed, forward = forward_side(at_whole, last_factor, middle_factor)
    forward_home = exchange(forward.reshape(tokens.shape))
    backward, last_part, middle_part = backward_side(
        sent_whole, at_whole, mixed, last_factor.transpose(0, 2, 1), middle_factor
    )
    back_home = exchange(backward.reshape(tokens.shape))
    gate_term, gate_part, first_part = close_side(
        tokens, cotangent, forward_home, gate_weight, first_factor
    )
    d_tokens = (back_home.astype(F32) + gate_term.astype(F32)).astype(BF16)
    return (d_tokens,) + reduced(
        gate_part, first_part, middle_part, last_part, 1.0 / math.sqrt(positions(tokens))
    )


def shards(tokens, *others):
    n_i, n_j, lanes, width = tokens.shape
    groups, blocks = lax.axis_size("grp"), lax.axis_size("seq")
    whole_tiles = lanes % 16 == 0 and n_j % 2 == 0 and blocks % 2 == 0
    if n_i == groups * blocks and whole_tiles and width % (HEADS * 128) == 0:
        return direct(tokens, *others)
    return general(tokens, *others)


def solution(mesh):
    in_specs = (P(None, "grp", "seq", None), P(None, "grp", "seq", None), P(), P(), P(), P())
    out_specs = (
        P(None, "grp", "seq", None),
        P("seq", None),
        P(),
        P(None, "grp", None),
        P(None, "seq", None),
    )
    return jax.shard_map(shards, mesh=mesh, in_specs=in_specs, out_specs=out_specs, check_vma=False)
```

time: 1820 us -> 875 us (0.48)
  blocking collectives: 832 us -> 58 us
  local copies, waits for them, and re-layouts: 363 us -> 0.77 us
  waiting for transfers between devices: 392 us -> 642 us
  matrix products: 164 us -> 0 us
  Pallas kernels: 0 us -> 126 us
    all_to_all x6 -> x0, blocking collectives: 781 us -> none  [the longest x2 379 us: send_last(): lax.all_to_all(values, 'seq', split_axis=0, concat_axis=2, tiled=True)]
    all_to_all x2 -> x4, waiting for transfers between devices: 171 us -> 473 us  [exchange(): return lax.all_to_all(values, ALL, split_axis=0, concat_axis=0, tiled=True)]
    unnamed x5 -> x4, waiting for transfers between devices: 189 us -> 1.41 us
    dot_general x12 -> x0, matrix products: 164 us -> none  [the longest x6 87.8 us: mixing(): jnp.einsum(form, weights, headed(values), preferred_element_type=jnp.floa...]
    convert_element_type x11 -> x0, local copies, waits for them, and re-layouts: 155 us -> none  [the longest x2 41.3 us: shards(): mixing(first_factor, tokens, 'hab,bjkhe->ajkhe').astype(jnp.bfloat16)]
    reduce_scatter x2 -> x3, waiting for transfers between devices: 0.02 us -> 136 us  [the longest x1 117 us: reduced(): lax.psum_scatter(last_part, 'seq', scatter_dimension=1, tiled=True)]
    pallas_call x0 -> x4, Pallas kernels: none -> 126 us  [the longest x1 48.2 us: backward_side(): pl.pallas_call(functools.partial(backward_kernel, groups, blocks, n_j, la...]
    all_to_all x10 -> x0, local copies, waits for them, and re-layouts: 107 us -> none  [the longest x3 27.9 us: return_middle(): lax.all_to_all(values, 'grp', split_axis=1, concat_axis=2, tiled=True)]
  transfers between devices with their start and end apart: 6 -> 8, of which waited for: 3 -> 7; matrix products, arithmetic and copies ran while one was open for 6% -> 2% of each run, Pallas kernels for 0% -> 14%
where the time goes in v1:
time: 875 us; the launch traced here: 874 us
  waiting for transfers between devices  642 us (73%)
  Pallas kernels  126 us (14%)
  blocking collectives  58 us (7%)
  starting transfers between devices  19 us (2%)
  other arithmetic  14.2 us (2%)
  between operations  13.8 us (2%)
    all_to_all x4, waiting for transfers between devices, exchange(): return lax.all_to_all(values, ALL, split_axis=0, concat_axis=0, tiled=True)  473 us
    reduce_scatter x1, waiting for transfers between devices, reduced(): lax.psum_scatter(last_part, 'seq', scatter_dimension=1, tiled=True)  117 us
    pallas_call x1, Pallas kernels, backward_side(): pl.pallas_call(functools.partial(backward_kernel, groups, blocks, n_j, la...  48.2 us
    psum x1, blocking collectives, reduced(): middle_sum, first_sum = lax.psum((middle_share, first_half), 'seq')  45.9 us
    psum x1, waiting for transfers between devices, reduced(): lax.psum((gate_share, last_share, first_part), 'grp')  32.3 us
    pallas_call x1, Pallas kernels, close_side(): pl.pallas_call(functools.partial(close_kernel, n_i, step_j, lanes, width)...  30.5 us
    pallas_call x1, Pallas kernels, forward_side(): pl.pallas_call(functools.partial(forward_kernel, groups, blocks, n_j, lan...  30.4 us
    all_to_all x4, starting transfers between devices, exchange(): return lax.all_to_all(values, ALL, split_axis=0, concat_axis=0, tiled=True)  18.7 us
  transfers between devices with their start and end apart: 8, of which 7 were waited for; matrix products, arithmetic and copies ran while one was open for 2% of the time, Pallas kernels for 14%

profile of v1, /device:TPU:0, one launch (start us, length us, event | category | flops | bytes accessed | tf_op | source)
XLA Modules:
  0.0 874.2 jit_solution(11826999269099368731)
XLA Ops:
  7.2 7.5 all-to-all-start.1
  14.6 16.9 %open_side.1 = bf16[32,16,16,512]{3,2,1,0:T(8,128)(2,1)} custom-call(bf16[32,16,16,512]{3,2,1,0:T(8,128)(2,1)} %x_ref.3, bf16[32,16,16,512]{3,2,1,0:T(8,128)(2,1)} %g_ref.3, bf16[512,512]{1,0:T(8,128)(2,1)} %w_ref.3, bf16[4,32,32]{2,1,0:T(8,128)(2,1)} %a_ref.3), custom_call_target="tpu_custom_call" | custom-call | flops 8589934592 | bytes 25165824 | tf_op jit(solution)/shard_map/open_side/pallas_call | solution.py:159
  31.6 172.9 %all-to-all-done.1 = bf16[32,16,16,512]{3,2,1,0:T(8,128)(2,1)} async-done(((bf16[32,16,16,512]{3,2,1,0:T(8,128)(2,1)}), bf16[32,16,16,512]{3,2,1,0:T(8,128)(2,1)}, u32[]{:S(2)}, u32[]{:S(2)}) %all-to-all-start.1) | async-done | bytes 8388640 | tf_op jit(solution)/shard_map/all_to_all | solution.py:92
  204.4 3.7 all-to-all-start
  208.2 30.4 %forward_side.1 = (bf16[4,8,16,16,512]{4,3,2,1,0:T(8,128)(2,1)}, bf16[4,8,16,16,512]{4,3,2,1,0:T(8,128)(2,1)}) custom-call(bf16[4,8,16,16,512]{4,3,2,1,0:T(8,128)(2,1)} %bitcast.1.x_ref, bf16[4,128,128]{2,1,0:T(8,128)(2,1)} %b_ref.1, bf16[4,64,64]{2,1,0:T(8,128)(2,1)} %c_ref.3), custom_call_target="tpu_custom_call" | custom-call | flops 9663676416 | bytes 25165824 | tf_op jit(solution)/shard_map/forward_side/pallas_call | solution.py:203
  238.5 159.2 %all-to-all-done = bf16[32,16,16,512]{3,2,1,0:T(8,128)(2,1)} async-done(((bf16[32,16,16,512]{3,2,1,0:T(8,128)(2,1)}), bf16[32,16,16,512]{3,2,1,0:T(8,128)(2,1)}, u32[]{:S(2)}, u32[]{:S(2)}) %all-to-all-start) | async-done | bytes 8388640 | tf_op jit(solution)/shard_map/all_to_all | solution.py:92
  397.8 3.8 all-to-all-start.3
  401.6 0.8 copy.11
  402.4 48.2 %backward_side.1 = (bf16[4,8,16,16,512]{4,3,2,1,0:T(8,128)(2,1)}, f32[4,128,128]{2,1,0:T(8,128)}, f32[4,64,64]{2,1,0:T(8,128)}) custom-call(bf16[4,8,16,16,512]{4,3,2,1,0:T(8,128)(2,1)} %bitcast.v_ref, bf16[4,8,16,16,512]{4,3,2,1,0:T(8,128)(2,1)} %bitcast.1.x_ref, bf16[4,8,16,16,512]{4,3,2,1,0:T(8,128)(2,1)} %get-tuple-element.13.bx_ref, ...), custom_call_target="tpu_custom_call" | custom-call | flops 19327352832 | bytes 33554432 | tf_op jit(solution)/shard_map/backward_side/pallas_call | solution.py:261
  450.5 140.7 %all-to-all-done.3.y_ref = bf16[32,16,16,512]{3,2,1,0:T(8,128)(2,1)} async-done(((bf16[32,16,16,512]{3,2,1,0:T(8,128)(2,1)}), bf16[32,16,16,512]{3,2,1,0:T(8,128)(2,1)}, u32[]{:S(2)}, u32[]{:S(2)}) %all-to-all-start.3) | async-done | bytes 8388640 | tf_op jit(solution)/shard_map/all_to_all | solution.py:92
  591.2 3.7 all-to-all-start.2
  594.9 0.0 reduce-scatter.8.cloned.1.call-start
  595.0 0.7 reduce-scatter.8.cloned.1.call-update
  595.7 0.0 reduce-scatter.6.cloned.1.call-start
  595.7 0.7 reduce-scatter.6.cloned.1.call-update
  596.4 0.2 reduce-scatter.4.cloned.1.call-start
  596.6 30.5 %close_side.1 = (bf16[32,16,16,512]{3,2,1,0:T(8,128)(2,1)}, f32[512,512]{1,0:T(8,128)}, f32[4,32,32]{2,1,0:T(8,128)}) custom-call(bf16[32,16,16,512]{3,2,1,0:T(8,128)(2,1)} %x_ref.3, bf16[32,16,16,512]{3,2,1,0:T(8,128)(2,1)} %g_ref.3, bf16[32,16,16,512]{3,2,1,0:T(8,128)(2,1)} %all-to-all-done.3.y_ref, bf16[512,512]{1,0:T(8,128)(2,1)} %w_ref.3, ...), custom_call_target="tpu_custom_call" | custom-call | flops 21474836480 | bytes 33554432 | tf_op jit(solution)/shard_map/close_side/pallas_call | solution.py:330
  627.2 0.0 reduce-scatter.4.cloned.1.call-update
  627.2 0.0 all-reduce.4.cloned.1.call-start
  627.3 116.6 %reduce-scatter.8.cloned.1.call-done = f32[4,16,128]{2,1,0:T(8,128)} async-done(((f32[4,128,128]{2,1,0:T(8,128)}), f32[4,16,128]{2,1,0:T(8,128)}) %reduce-scatter.8.cloned.1.call-update) | async-done | bytes 32784 | tf_op jit(solution)/shard_map/reduce_scatter | solution.py:84
  743.9 12.1 %all-reduce.1 = (f32[4,32,32]{2,1,0:T(8,128)S(1)}, f32[4,16,128]{2,1,0:T(8,128)S(1)}) all-reduce(f32[4,32,32]{2,1,0:T(8,128)} %get-tuple-element.18, f32[4,16,128]{2,1,0:T(8,128)} %reduce-scatter.8.cloned.1.call-done), channel_id=1, replica_groups=mesh['grp'=4,'seq'=8] {'grp'}, use_global_device_ids=true, to_apply=%region_2.0 | all-reduce | flops 12288 | bytes 98304 | tf_op jit(solution)/shard_map/psum | solution.py:86
  756.0 7.3 reduce-scatter.6.cloned.1.call-done
  763.3 45.9 %all-reduce = (f32[4,32,32]{2,1,0:T(8,128)S(1)}, f32[4,16,64]{2,1,0:T(8,128)S(1)}) all-reduce(f32[4,32,32]{2,1,0:T(8,128)S(1)} %get-tuple-element.23, f32[4,16,64]{2,1,0:T(8,128)} %reduce-scatter.6.cloned.1.call-done), channel_id=1, replica_groups=mesh['grp'=4,'seq'=8] {'seq'}, use_global_device_ids=true, to_apply=%region_3.0 | all-reduce | flops 8192 | bytes 65536 | tf_op jit(solution)/shard_map/psum | solution.py:87
  809.3 0.6 broadcast_multiply_fusion.3
  809.9 0.6 broadcast_multiply_fusion.1
  810.5 0.0 all-to-all-done.2
  810.5 10.7 %add_convert_fusion = bf16[32,16,16,512]{3,2,1,0:T(8,128)(2,1)} fusion(bf16[32,16,16,512]{3,2,1,0:T(8,128)(2,1)} %get-tuple-element.16, bf16[32,16,16,512]{3,2,1,0:T(8,128)(2,1)} %all-to-all-done.2), kind=kLoop, calls=%fused_computation | loop fusion | flops 16777216 | bytes 25165824 | tf_op jit(solution)/shard_map/convert_element_type | solution.py:368
  821.2 11.9 %reduce-scatter.4.cloned.1.call-done = f32[64,512]{1,0:T(8,128)} async-done(((f32[512,512]{1,0:T(8,128)}), f32[64,512]{1,0:T(8,128)}) %reduce-scatter.4.cloned.1.call-update) | async-done | bytes 131088 | tf_op jit(solution)/shard_map/reduce_scatter | solution.py:83
  833.2 0.0 all-reduce.4.cloned.1.call-update
  833.2 0.6 broadcast_multiply_fusion.2
  833.8 32.3 %all-reduce.4.cloned.1.call-done = f32[64,512]{1,0:T(8,128)} async-done(((f32[64,512]{1,0:T(8,128)}), f32[64,512]{1,0:T(8,128)}) %all-reduce.4.cloned.1.call-update) | async-done | bytes 131088 | tf_op jit(solution)/shard_map/psum | solution.py:86
  866.1 1.6 broadcast_multiply_fusion
  (2 shorter events, 0.0 us)
Async XLA Ops:
  7.2 197.3 %all-to-all-start.1 = ((bf16[32,16,16,512]{3,2,1,0:T(8,128)(2,1)}), bf16[32,16,16,512]{3,2,1,0:T(8,128)(2,1)}, u32[]{:S(2)}, u32[]{:S(2)}) async-start(bf16[32,16,16,512]{3,2,1,0:T(8,128)(2,1)} %x_ref.3), calls=%async_computation.1 | async-start | bytes 16777216 | tf_op jit(solution)/shard_map/all_to_all | solution.py:92
  204.4 193.3 %all-to-all-start = ((bf16[32,16,16,512]{3,2,1,0:T(8,128)(2,1)}), bf16[32,16,16,512]{3,2,1,0:T(8,128)(2,1)}, u32[]{:S(2)}, u32[]{:S(2)}) async-start(bf16[32,16,16,512]{3,2,1,0:T(8,128)(2,1)} %open_side.1), calls=%async_computation | async-start | bytes 16777216 | tf_op jit(solution)/shard_map/all_to_all | solution.py:92
  397.8 3.8 copy-start
  397.8 193.4 %all-to-all-start.3 = ((bf16[32,16,16,512]{3,2,1,0:T(8,128)(2,1)}), bf16[32,16,16,512]{3,2,1,0:T(8,128)(2,1)}, u32[]{:S(2)}, u32[]{:S(2)}) async-start(bf16[32,16,16,512]{3,2,1,0:T(8,128)(2,1)} %bitcast.6), calls=%async_computation.3 | async-start | bytes 16777216 | tf_op jit(solution)/shard_map/all_to_all | solution.py:92
  591.2 219.3 %all-to-all-start.2 = ((bf16[32,16,16,512]{3,2,1,0:T(8,128)(2,1)}), bf16[32,16,16,512]{3,2,1,0:T(8,128)(2,1)}, u32[]{:S(2)}, u32[]{:S(2)}) async-start(bf16[32,16,16,512]{3,2,1,0:T(8,128)(2,1)} %bitcast.5), calls=%async_computation.2 | async-start | bytes 16777216 | tf_op jit(solution)/shard_map/all_to_all | solution.py:92
  594.9 149.0 %reduce-scatter.8.cloned.1.call-start = ((), (), s32[]{:S(2)}) async-start(), calls=%async_computation.10 | async-start | bytes 294912 | tf_op jit(solution)/shard_map/reduce_scatter | solution.py:84
  595.7 167.7 %reduce-scatter.6.cloned.1.call-start = ((), (), s32[]{:S(2)}) async-start(), calls=%async_computation.9 | async-start | bytes 163840 | tf_op jit(solution)/shard_map/reduce_scatter | solution.py:85
  596.4 236.8 %reduce-scatter.4.cloned.1.call-start = ((), (), s32[]{:S(2)}) async-start(), calls=%async_computation.7 | async-start | bytes 1179648 | tf_op jit(solution)/shard_map/reduce_scatter | solution.py:83
  627.2 238.9 %all-reduce.4.cloned.1.call-start = ((), (), s32[]{:S(2)}) async-start(), calls=%async_computation.8 | async-start | bytes 262144 | tf_op jit(solution)/shard_map/psum | solution.py:86
Sparse Core Ops, SparseCore 0:
  599.1 144.7 reduce-scatter.7
  746.3 16.9 reduce-scatter.5
  766.7 66.4 reduce-scatter.3
  835.4 30.6 all-reduce.3

commit v2 on v1

--- a/solution.py
+++ b/solution.py
@@ -8,7 +8,9 @@
 from jax.experimental.pallas import tpu as pltpu
 from jax.sharding import PartitionSpec as P
 
+
 HEADS = 4
+EARLY = 3
 ALL = ("grp", "seq")
 F32 = jnp.float32
 BF16 = jnp.bfloat16
@@ -217,9 +219,11 @@
 
 
 def backward_kernel(
-    groups, blocks, n_j, lanes, size, v_ref, x_ref, bx_ref, b_ref, c_ref, u_ref, gl_ref, gm_ref, cv, acc, wide
+    groups, blocks, n_j, lanes, size, v_ref, x_ref, bx_ref, b_ref, c_ref, early_ref, late_ref, gl_ref,
+    gm_ref, cv, acc, wide
 ):
     rows = groups * n_j * lanes
+    is_early = pl.program_id(0) < EARLY
     wide[...] = spread(c_ref[0], lanes, turned=True)
     acc[...] = jnp.zeros_like(acc)
 
@@ -244,7 +248,16 @@
         held = [x_ref[g, :, j + p].reshape(blocks * lanes, size) for p in range(2)]
         out = dot(last, back).astype(BF16)
         for p in range(2):
-            u_ref[g, :, j + p] = out[:, p * size : (p + 1) * size].reshape(blocks, lanes, size)
+            piece = out[:, p * size : (p + 1) * size].reshape(blocks, lanes, size)
+
+            @pl.when(is_early)
+            def _():
+                early_ref[g, :, j + p] = piece
+
+            @pl.when(jnp.logical_not(is_early))
+            def _():
+                late_ref[g, :, j + p] = piece
+
         return total + dot_rows(back, jnp.concatenate(held, axis=1))
 
     zero = jnp.zeros((blocks * lanes, blocks * lanes), F32)
@@ -262,9 +275,15 @@
         functools.partial(backward_kernel, groups, blocks, n_j, lanes, size),
         grid=(HEADS,),
         in_specs=[block] * 3 + [one(n_last, n_last), one(n_middle, n_middle)],
-        out_specs=[block, one(n_last, n_last), one(n_middle, n_middle)],
+        out_specs=[
+            pl.BlockSpec(block.block_shape, lambda h: (0, 0, 0, 0, jnp.minimum(h, EARLY - 1))),
+            pl.BlockSpec(block.block_shape, lambda h: (0, 0, 0, 0, jnp.maximum(h - EARLY, 0))),
+            one(n_last, n_last),
+            one(n_middle, n_middle),
+        ],
         out_shape=[
-            jax.ShapeDtypeStruct(values.shape, BF16),
+            jax.ShapeDtypeStruct(values.shape[:-1] + (EARLY * size,), BF16),
+            jax.ShapeDtypeStruct(values.shape[:-1] + (width - EARLY * size,), BF16),
             jax.ShapeDtypeStruct((HEADS, n_last, n_last), F32),
             jax.ShapeDtypeStruct((HEADS, n_middle, n_middle), F32),
         ],
@@ -350,7 +369,128 @@
     )(tokens, cotangent, mixed, gate_weight, first_factor)
 
 
-def direct(tokens, cotangent, gate_weight, first_factor, middle_factor, last_factor):
+def finish_kernel(b_ref, t_ref, *refs):
+    refs[-1][...] = (b_ref[...].astype(F32) + t_ref[...].astype(F32)).astype(BF16)
+
+
+def finish(back, gate_term, offset, held=None):
+    n_i, n_j, lanes, width = gate_term.shape
+    size = width // HEADS
+    step = n_i // 4
+    here = pl.BlockSpec((step, n_j, lanes, size), lambda h, i: (i, 0, 0, h))
+    there = pl.BlockSpec((step, n_j, lanes, size), lambda h, i: (i, 0, 0, h + offset))
+    more = [] if held is None else [held]
+    return pl.pallas_call(
+        finish_kernel,
+        grid=(back.shape[-1] // size, n_i // step),
+        in_specs=[here, there] + [pl.BlockSpec(memory_space=pl.ANY)] * len(more),
+        out_specs=there,
+        out_shape=jax.ShapeDtypeStruct(gate_term.shape, BF16),
+        input_output_aliases={2: 0} if more else {},
+        cost_estimate=pl.CostEstimate(flops=back.size, bytes_accessed=6 * back.size, transcendentals=0),
+    )(back, gate_term, *more)
+
+
+def shifted(parts, axis):
+    count = lax.axis_size(axis)
+    me = lax.axis_index(axis)
+    out = []
+    for d in range(1, count):
+        part = lax.dynamic_index_in_dim(parts, (me + d) % count, 0, False)
+        out.append(lax.ppermute(part, axis, [(i, (i + d) % count) for i in range(count)]))
+    return out
+
+
+def share_kernel(factor, *refs):
+    total = refs[0][...]
+    for part in refs[1:-1]:
+        total += part[...]
+    refs[-1][...] = total * factor
+
+
+def share_sum(parts, factor):
+    return pl.pallas_call(
+        functools.partial(share_kernel, factor),
+        out_shape=jax.ShapeDtypeStruct(parts[0].shape, F32),
+        name="share_sum",
+    )(*parts)
+
+
+def ordered_kernel(axis, *refs):
+    parts, out_ref, held = refs[:-2], refs[-2], refs[-1]
+    count = len(parts)
+    me = lax.axis_index(axis)
+    for d, part in enumerate(parts):
+        held[d] = part[...]
+    total = held[lax.rem(me + count, count)]
+    for source in range(1, count):
+        total += held[lax.rem(me - source + count, count)]
+    out_ref[...] = total
+
+
+def ordered_sum(parts, axis):
+    shape = parts[0].shape
+    return pl.pallas_call(
+        functools.partial(ordered_kernel, axis),
+        out_shape=jax.ShapeDtypeStruct(shape, F32),
+        scratch_shapes=[pltpu.VMEM((len(parts),) + shape, F32)],
+        name="ordered_sum",
+    )(*parts)
+
+
+def reduced_direct(gate_part, first_part, middle_part, last_part, factor):
+    groups, blocks = lax.axis_size("grp"), lax.axis_size("seq")
+    width = gate_part.shape[0]
+    n_last, n_middle, n_first = last_part.shape[1], middle_part.shape[1], first_part.shape[1]
+    lane = width // groups
+    own = HEADS // groups
+
+    def flat(parts):
+        return parts.reshape(parts.shape[0], -1, lane)
+
+    packed = jnp.concatenate(
+        [
+            gate_part.reshape(width, groups, lane).transpose(1, 0, 2),
+            flat(last_part.reshape(groups, -1)),
+            flat(middle_part.reshape(HEADS, groups, -1).transpose(1, 0, 2)),
+            flat(first_part.reshape(groups, -1)),
+        ],
+        axis=1,
+    )
+    mine = lax.dynamic_index_in_dim(packed, lax.axis_index("grp"), 0, False)
+    share = share_sum([mine] + shifted(packed, "grp"), factor)
+    cuts = [width, own * n_last * n_last // lane, HEADS * n_middle * n_middle // groups // lane]
+    gate, last, middle, first = jnp.split(share, [sum(cuts[: n + 1]) for n in range(3)])
+    last = last.reshape(own, blocks, n_last // blocks, n_last).transpose(1, 0, 2, 3)
+    again = jnp.concatenate(
+        [
+            gate.reshape(blocks, -1, lane),
+            flat(last.reshape(blocks, -1)),
+            jnp.broadcast_to(middle, (blocks,) + middle.shape),
+            jnp.broadcast_to(first, (blocks,) + first.shape),
+        ],
+        axis=1,
+    )
+    mine = lax.dynamic_index_in_dim(again, lax.axis_index("seq"), 0, False)
+    total = ordered_sum([mine] + shifted(again, "seq"), "seq")
+    cuts = [width // blocks, own * n_last * n_last // blocks // lane, middle.shape[0]]
+    gate, last, middle, first = jnp.split(total, [sum(cuts[: n + 1]) for n in range(3)])
+    give = jnp.concatenate([gate, last, first])
+    me = lax.axis_index("grp")
+    spread_out = jnp.zeros((groups,) + give.shape, F32)
+    spread_out = lax.dynamic_update_index_in_dim(spread_out, give, me, 0)
+    for d, part in enumerate(shifted(jnp.broadcast_to(give, (groups,) + give.shape), "grp"), 1):
+        spread_out = lax.dynamic_update_index_in_dim(spread_out, part, (me - d) % groups, 0)
+    gate, last, first = jnp.split(spread_out, [gate.shape[0], gate.shape[0] + last.shape[0]], axis=1)
+    return (
+        gate.transpose(1, 0, 2).reshape(-1, width),
+        first.reshape(HEADS, n_first, n_first),
+        middle.reshape(HEADS, n_middle // groups, n_middle),
+        last.reshape(HEADS, n_last // blocks, n_last),
+    )
+
+
+def ordered(tokens, cotangent, gate_weight, first_factor, middle_factor, last_factor):
     groups, blocks = lax.axis_size("grp"), lax.axis_size("seq")
     split = (groups, blocks) + tokens.shape[1:]
     at_whole = exchange(tokens).reshape(split)
@@ -358,25 +498,28 @@
     sent_whole = exchange(sent).reshape(split)
     mixed, forward = forward_side(at_whole, last_factor, middle_factor)
     forward_home = exchange(forward.reshape(tokens.shape))
-    backward, last_part, middle_part = backward_side(
+    early, late, last_part, middle_part = backward_side(
         sent_whole, at_whole, mixed, last_factor.transpose(0, 2, 1), middle_factor
     )
-    back_home = exchange(backward.reshape(tokens.shape))
+    early_home = exchange(early.reshape(tokens.shape[:-1] + early.shape[-1:]))
     gate_term, gate_part, first_part = close_side(
         tokens, cotangent, forward_home, gate_weight, first_factor
     )
-    d_tokens = (back_home.astype(F32) + gate_term.astype(F32)).astype(BF16)
-    return (d_tokens,) + reduced(
+    sums = reduced_direct(
         gate_part, first_part, middle_part, last_part, 1.0 / math.sqrt(positions(tokens))
     )
+    late_home = exchange(late.reshape(tokens.shape[:-1] + late.shape[-1:]))
+    d_tokens = finish(early_home, gate_term, 0)
+    return (finish(late_home, gate_term, EARLY, d_tokens),) + sums
 
 
 def shards(tokens, *others):
     n_i, n_j, lanes, width = tokens.shape
     groups, blocks = lax.axis_size("grp"), lax.axis_size("seq")
     whole_tiles = lanes % 16 == 0 and n_j % 2 == 0 and blocks % 2 == 0
-    if n_i == groups * blocks and whole_tiles and width % (HEADS * 128) == 0:
-        return direct(tokens, *others)
+    lane_sized = width == groups * 128 and HEADS % groups == 0
+    if n_i == groups * blocks and whole_tiles and lane_sized and n_i % 4 == 0 and width % (HEADS * 128) == 0:
+        return ordered(tokens, *others)
     return general(tokens, *others)
 
 

time: 875 us -> 897 us (1.025)
  waiting for transfers between devices: 642 us -> 350 us
  blocking collectives: 58 us -> 331 us
  Pallas kernels: 126 us -> 168 us
  local copies, waits for them, and re-layouts: 0.77 us -> 14.9 us
  other arithmetic: 14.2 us -> 0.15 us
  between operations: 13.8 us -> 0.93 us
  starting transfers between devices: 19 us -> 30.3 us
    all_to_all x0 -> x2, blocking collectives: none -> 331 us  [exchange(): return lax.all_to_all(values, ALL, split_axis=0, concat_axis=0, tiled=True)]
    all_to_all x4 -> x3, waiting for transfers between devices: 473 us -> 331 us  [exchange(): return lax.all_to_all(values, ALL, split_axis=0, concat_axis=0, tiled=True)]
    reduce_scatter x3 -> x0, waiting for transfers between devices: 136 us -> none  [the longest x1 117 us: reduced(): lax.psum_scatter(last_part, 'seq', scatter_dimension=1, tiled=True)]
    psum x2 -> x0, blocking collectives: 58 us -> none  [the longest x1 45.9 us: reduced(): middle_sum, first_sum = lax.psum((middle_share, first_half), 'seq')]
    psum x1 -> x0, waiting for transfers between devices: 32.3 us -> none  [reduced(): lax.psum((gate_share, last_share, first_part), 'grp')]
    pallas_call x1, Pallas kernels: 48.2 us -> 70.5 us  [backward_side(): pl.pallas_call(functools.partial(backward_kernel, groups, blocks, n_j, la...]
    pallas_call x0 -> x4, Pallas kernels: none -> 19.5 us  [the longest x2 15.7 us: finish(): pl.pallas_call(finish_kernel, grid=(back.shape[-1] // size, n_i // step),...]
    ppermute x0 -> x13, waiting for transfers between devices: none -> 18.4 us  [shifted(): lax.ppermute(part, axis, [(i, (i + d) % count) for i in range(count)])]
  transfers between devices with their start and end apart: 8 -> 16, of which waited for: 7 -> 6; matrix products, arithmetic and copies ran while one was open for 2% -> 1% of each run, Pallas kernels for 14% -> 11%
where the time goes in v2:
time: 897 us; the launch traced here: 895 us
  waiting for transfers between devices  350 us (39%)
  blocking collectives  331 us (37%)
  Pallas kernels  168 us (19%)
  starting transfers between devices  30.3 us (3%)
  local copies, waits for them, and re-layouts  14.9 us (2%)
    all_to_all x3, waiting for transfers between devices, exchange(): return lax.all_to_all(values, ALL, split_axis=0, concat_axis=0, tiled=True)  331 us
    all_to_all x2, blocking collectives, exchange(): return lax.all_to_all(values, ALL, split_axis=0, concat_axis=0, tiled=True)  331 us
    pallas_call x1, Pallas kernels, backward_side(): pl.pallas_call(functools.partial(backward_kernel, groups, blocks, n_j, la...  70.5 us
    pallas_call x1, Pallas kernels, close_side(): pl.pallas_call(functools.partial(close_kernel, n_i, step_j, lanes, width)...  30.5 us
    pallas_call x1, Pallas kernels, forward_side(): pl.pallas_call(functools.partial(forward_kernel, groups, blocks, n_j, lan...  30.3 us
    ppermute x13, waiting for transfers between devices, shifted(): lax.ppermute(part, axis, [(i, (i + d) % count) for i in range(count)])  18.4 us
  transfers between devices with their start and end apart: 16, of which 6 were waited for; matrix products, arithmetic and copies ran while one was open for 1% of the time, Pallas kernels for 11%

profile of v2, /device:TPU:0, one launch (start us, length us, event | category | flops | bytes accessed | tf_op | source)
XLA Modules:
  0.0 895.1 jit_solution(14817695575349579187)
XLA Ops:
  0.6 7.5 all-to-all-start.1
  8.1 16.9 %open_side.1 = bf16[32,16,16,512]{3,2,1,0:T(8,128)(2,1)} custom-call(bf16[32,16,16,512]{3,2,1,0:T(8,128)(2,1)} %x_ref.3, bf16[32,16,16,512]{3,2,1,0:T(8,128)(2,1)} %g_ref.3, bf16[512,512]{1,0:T(8,128)(2,1)} %w_ref.3, bf16[4,32,32]{2,1,0:T(8,128)(2,1)} %a_ref.3), custom_call_target="tpu_custom_call" | custom-call | flops 8589934592 | bytes 25165824 | tf_op jit(solution)/shard_map/open_side/pallas_call | solution.py:161
  25.0 172.9 %all-to-all-done.1 = bf16[32,16,16,512]{3,2,1,0:T(8,128)(2,1)} async-done(((bf16[32,16,16,512]{3,2,1,0:T(8,128)(2,1)}), bf16[32,16,16,512]{3,2,1,0:T(8,128)(2,1)}, u32[]{:S(2)}, u32[]{:S(2)}) %all-to-all-start.1) | async-done | bytes 8388640 | tf_op jit(solution)/shard_map/all_to_all | solution.py:94
  197.9 3.7 all-to-all-start
  202.4 30.3 %forward_side.1 = (bf16[4,8,16,16,512]{4,3,2,1,0:T(8,128)(2,1)}, bf16[4,8,16,16,512]{4,3,2,1,0:T(8,128)(2,1)}) custom-call(bf16[4,8,16,16,512]{4,3,2,1,0:T(8,128)(2,1)} %bitcast.1.x_ref, bf16[4,128,128]{2,1,0:T(8,128)(2,1)} %b_ref.1, bf16[4,64,64]{2,1,0:T(8,128)(2,1)} %c_ref.3), custom_call_target="tpu_custom_call" | custom-call | flops 9663676416 | bytes 25165824 | tf_op jit(solution)/shard_map/forward_side/pallas_call | solution.py:205
  232.7 158.5 %all-to-all-done = bf16[32,16,16,512]{3,2,1,0:T(8,128)(2,1)} async-done(((bf16[32,16,16,512]{3,2,1,0:T(8,128)(2,1)}), bf16[32,16,16,512]{3,2,1,0:T(8,128)(2,1)}, u32[]{:S(2)}, u32[]{:S(2)}) %all-to-all-start) | async-done | bytes 8388640 | tf_op jit(solution)/shard_map/all_to_all | solution.py:94
  391.2 70.5 %backward_side.1 = (bf16[4,8,16,16,384]{4,3,2,1,0:T(8,128)(2,1)}, bf16[4,8,16,16,128]{4,3,2,1,0:T(8,128)(2,1)}, f32[4,128,128]{2,1,0:T(8,128)}, f32[4,64,64]{2,1,0:T(8,128)}) custom-call(bf16[4,8,16,16,512]{4,3,2,1,0:T(8,128)(2,1)} %bitcast.v_ref, bf16[4,8,16,16,512]{4,3,2,1,0:T(8,128)(2,1)} %bitcast.1.x_ref, ...), custom_call_target="tpu_custom_call" | custom-call | flops 19327352832 | bytes 33554432 | tf_op jit(solution)/shard_map/backward_side/pallas_call | solution.py:274
  461.7 143.9 %all_to_all.25.b_ref = bf16[32,16,16,384]{3,2,1,0:T(8,128)(2,1)} all-to-all(bf16[32,16,16,384]{3,2,1,0:T(8,128)(2,1)} %bitcast.55), channel_id=1, replica_groups=mesh['grp'=4,'seq'=8] {'grp','seq'}, dimensions={0} | all-to-all | bytes 12582912 | tf_op jit(solution)/shard_map/all_to_all | solution.py:94
  605.6 187.4 %all_to_all.26.y_ref = bf16[32,16,16,512]{3,2,1,0:T(8,128)(2,1)} all-to-all(bf16[32,16,16,512]{3,2,1,0:T(8,128)(2,1)S(1)} %bitcast.54), channel_id=1, replica_groups=mesh['grp'=4,'seq'=8] {'grp','seq'}, dimensions={0} | all-to-all | bytes 16777216 | tf_op jit(solution)/shard_map/all_to_all | solution.py:94
  793.0 2.9 all-to-all-start.2
  796.2 30.5 %close_side.1 = (bf16[32,16,16,512]{3,2,1,0:T(8,128)(2,1)}, f32[512,512]{1,0:T(8,128)}, f32[4,32,32]{2,1,0:T(8,128)}) custom-call(bf16[32,16,16,512]{3,2,1,0:T(8,128)(2,1)} %x_ref.3, bf16[32,16,16,512]{3,2,1,0:T(8,128)(2,1)} %g_ref.3, bf16[32,16,16,512]{3,2,1,0:T(8,128)(2,1)} %all_to_all.26.y_ref, bf16[512,512]{1,0:T(8,128)(2,1)} %w_ref.3, ...), custom_call_target="tpu_custom_call" | custom-call | flops 21474836480 | bytes 33554432 | tf_op jit(solution)/shard_map/close_side/pallas_call | solution.py:349
  826.7 0.9 reshape_reshape.3
  827.6 1.3 bitcast_bitcast_fusion
  829.9 1.6 collective-permute-start.1
  831.5 1.3 collective-permute-start.2
  832.8 9.0 %collective-permute-done.refs_1_ = f32[680,128]{1,0:T(8,128)S(1)} collective-permute-done((f32[680,128]{1,0:T(8,128)S(1)}, f32[680,128]{1,0:T(8,128)S(1)}, u32[]{:S(2)}, u32[]{:S(2)}) %collective-permute-start) | collective-permute-done | bytes 348192 | tf_op jit(solution)/shard_map/ppermute | solution.py:400
  841.8 1.6 collective-permute-done.1.refs_2_
  843.3 7.1 collective-permute-done.2.refs_3_
  850.4 2.1 share_sum.1
  854.8 1.0 split.41
  857.1 1.5 collective-permute-start.4
  858.6 1.8 collective-permute-start.5
  860.4 1.4 collective-permute-start.6
  861.8 2.1 collective-permute-start.7
  863.9 2.5 collective-permute-start.8
  866.4 1.2 collective-permute-start.9
  867.6 11.4 %shard_map.101.refs_0_ = bf16[32,16,16,512]{3,2,1,0:T(8,128)(2,1)} custom-call(bf16[32,16,16,384]{3,2,1,0:T(8,128)(2,1)} %all_to_all.25.b_ref, bf16[32,16,16,512]{3,2,1,0:T(8,128)(2,1)} %get-tuple-element.17.t_ref), custom_call_target="tpu_custom_call" | custom-call | flops 3145728 | bytes 18874368 | tf_op jit(solution)/shard_map/pallas_call | solution.py:383
  879.0 1.4 copy-done.1
  880.3 4.3 shard_map.102
  885.4 1.7 ordered_sum.1
  888.6 0.9 collective-permute-start.11
  889.5 1.4 collective-permute-start.12
  (66 shorter events, 11.9 us)
Async XLA Ops:
  0.6 197.3 %all-to-all-start.1 = ((bf16[32,16,16,512]{3,2,1,0:T(8,128)(2,1)}), bf16[32,16,16,512]{3,2,1,0:T(8,128)(2,1)}, u32[]{:S(2)}, u32[]{:S(2)}) async-start(bf16[32,16,16,512]{3,2,1,0:T(8,128)(2,1)} %x_ref.3), calls=%async_computation.1 | async-start | bytes 16777216 | tf_op jit(solution)/shard_map/all_to_all | solution.py:94
  25.0 176.6 %copy-start.5 = (bf16[4,128,128]{2,1,0:T(8,128)(2,1)S(1)}, bf16[4,128,128]{2,1,0:T(8,128)(2,1)}, u32[]{:S(2)}) copy-start(bf16[4,128,128]{2,1,0:T(8,128)(2,1)} %b_ref.1) | copy-start | bytes 393220
  197.9 193.3 %all-to-all-start = ((bf16[32,16,16,512]{3,2,1,0:T(8,128)(2,1)}), bf16[32,16,16,512]{3,2,1,0:T(8,128)(2,1)}, u32[]{:S(2)}, u32[]{:S(2)}) async-start(bf16[32,16,16,512]{3,2,1,0:T(8,128)(2,1)} %open_side.1), calls=%async_computation | async-start | bytes 16777216 | tf_op jit(solution)/shard_map/all_to_all | solution.py:94
  461.7 143.9 %copy-start = (bf16[4,8,16,16,512]{4,3,2,1,0:T(8,128)(2,1)S(1)}, bf16[4,8,16,16,512]{4,3,2,1,0:T(8,128)(2,1)}, u32[]{:S(2)}) copy-start(bf16[4,8,16,16,512]{4,3,2,1,0:T(8,128)(2,1)} %get-tuple-element.16) | copy-start | bytes 25165828
  605.6 190.4 %copy-start.4 = (f32[4,64,64]{2,1,0:T(8,128)S(1)}, f32[4,64,64]{2,1,0:T(8,128)}, u32[]{:S(2)}) copy-start(f32[4,64,64]{2,1,0:T(8,128)} %get-tuple-element.21) | copy-start | bytes 196612
  793.0 85.9 %all-to-all-start.2 = ((bf16[32,16,16,128]{3,2,1,0:T(8,128)(2,1)}), bf16[32,16,16,128]{3,2,1,0:T(8,128)(2,1)S(1)}, u32[]{:S(2)}, u32[]{:S(2)}) async-start(bf16[32,16,16,128]{3,2,1,0:T(8,128)(2,1)} %bitcast.56), calls=%async_computation.2 | async-start | bytes 4194304 | tf_op jit(solution)/shard_map/all_to_all | solution.py:94
  796.2 32.7 %copy-start.3 = (f32[4,128,128]{2,1,0:T(8,128)S(1)}, f32[4,128,128]{2,1,0:T(8,128)}, u32[]{:S(2)}) copy-start(f32[4,128,128]{2,1,0:T(8,128)} %get-tuple-element.20) | copy-start | bytes 786436
  829.9 11.9 %collective-permute-start = (f32[680,128]{1,0:T(8,128)S(1)}, f32[680,128]{1,0:T(8,128)S(1)}, u32[]{:S(2)}, u32[]{:S(2)}) collective-permute-start(f32[680,128]{1,0:T(8,128)S(1)} %get-tuple-element.25), channel_id=1, source_target_pairs={{0,8},{8,16},{16,24},{24,0},{1,9},{9,17},{17,25},{25,1},{2,10},{10... | collective-permute-start | bytes 1044488 | tf_op jit(solution)/shard_map/ppermute | solution.py:400
  829.9 13.4 %collective-permute-start.1 = (f32[680,128]{1,0:T(8,128)S(1)}, f32[680,128]{1,0:T(8,128)}, u32[]{:S(2)}, u32[]{:S(2)}) collective-permute-start(f32[680,128]{1,0:T(8,128)S(1)} %get-tuple-element.24), channel_id=1, source_target_pairs={{0,16},{8,24},{16,0},{24,8},{1,17},{9,25},{17,1},{25,9},{2,18},{10... | collective-permute-start | bytes 1044488 | tf_op jit(solution)/shard_map/ppermute | solution.py:400
  831.5 19.0 %collective-permute-start.2 = (f32[680,128]{1,0:T(8,128)S(1)}, f32[680,128]{1,0:T(8,128)}, u32[]{:S(2)}, u32[]{:S(2)}) collective-permute-start(f32[680,128]{1,0:T(8,128)S(1)} %get-tuple-element.23), channel_id=1, source_target_pairs={{0,24},{8,0},{16,8},{24,16},{1,25},{9,1},{17,9},{25,17},{2,26},{10... | collective-permute-start | bytes 1044488 | tf_op jit(solution)/shard_map/ppermute | solution.py:400
  841.8 8.7 copy-start.2
  856.5 7.4 collective-permute-start.3
  857.1 9.3 %collective-permute-start.4 = (f32[120,128]{1,0:T(8,128)S(1)}, f32[120,128]{1,0:T(8,128)S(1)}, u32[]{:S(2)}, u32[]{:S(2)}) collective-permute-start(f32[120,128]{1,0:T(8,128)S(1)} %get-tuple-element.32), channel_id=1, source_target_pairs={{0,2},{1,3},{2,4},{3,5},{4,6},{5,7},{6,0},{7,1},{8,10},{9,11},{10,... | collective-permute-start | bytes 184328 | tf_op jit(solution)/shard_map/ppermute | solution.py:400
  858.6 26.0 %collective-permute-start.5 = (f32[120,128]{1,0:T(8,128)S(1)}, f32[120,128]{1,0:T(8,128)S(1)}, u32[]{:S(2)}, u32[]{:S(2)}) collective-permute-start(f32[120,128]{1,0:T(8,128)S(1)} %get-tuple-element.31), channel_id=1, source_target_pairs={{0,3},{1,4},{2,5},{3,6},{4,7},{5,0},{6,1},{7,2},{8,11},{9,12},{10,... | collective-permute-start | bytes 184328 | tf_op jit(solution)/shard_map/ppermute | solution.py:400
  860.4 24.3 %collective-permute-start.6 = (f32[120,128]{1,0:T(8,128)S(1)}, f32[120,128]{1,0:T(8,128)S(1)}, u32[]{:S(2)}, u32[]{:S(2)}) collective-permute-start(f32[120,128]{1,0:T(8,128)S(1)} %get-tuple-element.30), channel_id=1, source_target_pairs={{0,4},{1,5},{2,6},{3,7},{4,0},{5,1},{6,2},{7,3},{8,12},{9,13},{10,... | collective-permute-start | bytes 184328 | tf_op jit(solution)/shard_map/ppermute | solution.py:400
  861.8 22.9 %collective-permute-start.7 = (f32[120,128]{1,0:T(8,128)S(1)}, f32[120,128]{1,0:T(8,128)S(1)}, u32[]{:S(2)}, u32[]{:S(2)}) collective-permute-start(f32[120,128]{1,0:T(8,128)S(1)} %get-tuple-element.29), channel_id=1, source_target_pairs={{0,5},{1,6},{2,7},{3,0},{4,1},{5,2},{6,3},{7,4},{8,13},{9,14},{10,... | collective-permute-start | bytes 184328 | tf_op jit(solution)/shard_map/ppermute | solution.py:400
  863.9 15.1 %copy-start.6 = (f32[120,128]{1,0:T(8,128)}, f32[120,128]{1,0:T(8,128)S(1)}, u32[]{:S(2)}) copy-start(f32[120,128]{1,0:T(8,128)S(1)} %collective-permute-done.3.refs_1_) | copy-start | bytes 184324
  863.9 20.8 %collective-permute-start.8 = (f32[120,128]{1,0:T(8,128)S(1)}, f32[120,128]{1,0:T(8,128)S(1)}, u32[]{:S(2)}, u32[]{:S(2)}) collective-permute-start(f32[120,128]{1,0:T(8,128)S(1)} %get-tuple-element.28), channel_id=1, source_target_pairs={{0,6},{1,7},{2,0},{3,1},{4,2},{5,3},{6,4},{7,5},{8,14},{9,15},{10,... | collective-permute-start | bytes 184328 | tf_op jit(solution)/shard_map/ppermute | solution.py:400
  866.4 12.6 %copy-start.7 = (f32[120,128]{1,0:T(8,128)}, f32[120,128]{1,0:T(8,128)S(1)}, u32[]{:S(2)}) copy-start(f32[120,128]{1,0:T(8,128)S(1)} %collective-permute-done.4.refs_2_) | copy-start | bytes 184324
  866.4 18.3 %collective-permute-start.9 = (f32[120,128]{1,0:T(8,128)S(1)}, f32[120,128]{1,0:T(8,128)S(1)}, u32[]{:S(2)}, u32[]{:S(2)}) collective-permute-start(f32[120,128]{1,0:T(8,128)S(1)} %get-tuple-element.27), channel_id=1, source_target_pairs={{0,7},{1,0},{2,1},{3,2},{4,3},{5,4},{6,5},{7,6},{8,15},{9,8},{10,9... | collective-permute-start | bytes 184328 | tf_op jit(solution)/shard_map/ppermute | solution.py:400
  879.0 1.4 copy-start.1
  884.7 0.6 copy-start.8
  884.7 0.6 copy-start.9
  884.7 0.6 copy-start.10
  884.7 0.6 copy-start.11
  884.7 0.7 copy-start.12
  888.6 3.7 collective-permute-start.10
  888.6 4.5 collective-permute-start.11
  889.5 3.6 collective-permute-start.12

commit v3 on v2

v3 whole, which is shorter than its diff:
```python
import functools
import math

import jax
import jax.numpy as jnp
from jax import lax
from jax.experimental import pallas as pl
from jax.experimental.pallas import tpu as pltpu
from jax.sharding import PartitionSpec as P


HEADS = 4
F32 = jnp.float32
BF16 = jnp.bfloat16


def headed(values):
    return values.reshape(values.shape[:-1] + (HEADS, values.shape[-1] // HEADS))


def mixing(weights, values, form):
    result = jnp.einsum(form, weights, headed(values), preferred_element_type=F32)
    return result.reshape(values.shape)


def contract(left, right, form):
    return jnp.einsum(form, headed(left), headed(right), preferred_element_type=F32)


def send_last(values):
    return lax.all_to_all(values, "seq", split_axis=0, concat_axis=2, tiled=True)


def send_middle(values):
    return lax.all_to_all(values, "grp", split_axis=2, concat_axis=1, tiled=True)


def return_middle(values):
    return lax.all_to_all(values, "grp", split_axis=1, concat_axis=2, tiled=True)


def return_last(values):
    return lax.all_to_all(values, "seq", split_axis=2, concat_axis=0, tiled=True)


def positions(tokens, seq):
    return math.prod(tokens.shape[:3]) * lax.axis_size("grp") * lax.axis_size(seq)


def general(tokens, cotangent, gate_weight, first_factor, middle_factor, last_factor):
    width = tokens.shape[-1]
    rows = tokens.reshape(-1, width)
    gate = jax.nn.sigmoid(jnp.dot(rows, gate_weight, preferred_element_type=F32))
    gate = gate.reshape(tokens.shape)
    first_out = mixing(first_factor, tokens, "hab,bjkhe->ajkhe").astype(BF16)
    last_in = send_last(first_out)
    last_out = mixing(last_factor, last_in, "hab,ijbhe->ijahe").astype(BF16)
    middle_in = send_middle(last_out)
    middle_out = mixing(middle_factor, middle_in, "hab,ibkhe->iakhe").astype(BF16)
    mixer = return_last(return_middle(middle_out))
    upstream = cotangent.astype(F32)
    d_mix = (upstream * gate).astype(BF16)
    d_pre = (upstream * mixer.astype(F32) * gate * (1.0 - gate)).astype(BF16)
    pre_rows = d_pre.reshape(-1, width)
    gate_part = jnp.einsum("tc,td->cd", rows, pre_rows, preferred_element_type=F32)
    gate_term = jnp.einsum("td,cd->tc", pre_rows, gate_weight, preferred_element_type=F32)
    middle_grad_in = send_middle(send_last(d_mix))
    middle_back = mixing(middle_factor, middle_grad_in, "hba,ibkhe->iakhe").astype(BF16)
    middle_part = contract(middle_grad_in, middle_in, "iakhe,ibkhe->hab")
    last_back_in = return_middle(middle_back)
    last_back = mixing(last_factor, last_back_in, "hba,ijbhe->ijahe").astype(BF16)
    last_part = contract(last_back_in, last_in, "ijahe,ijbhe->hab")
    first_back_in = return_last(last_back)
    first_back = mixing(first_factor, first_back_in, "hba,bjkhe->ajkhe")
    first_part = contract(first_back_in, tokens, "ajkhe,bjkhe->hab")
    d_tokens = (first_back.reshape(-1, width) + gate_term).astype(BF16).reshape(tokens.shape)
    return (d_tokens,) + reduced(
        gate_part, first_part, middle_part, last_part, 1.0 / math.sqrt(positions(tokens, "seq"))
    )


def reduced(gate_part, first_part, middle_part, last_part, factor):
    gate_share = lax.psum_scatter(gate_part, "seq", scatter_dimension=0, tiled=True)
    last_share = lax.psum_scatter(last_part, "seq", scatter_dimension=1, tiled=True)
    middle_share = lax.psum_scatter(middle_part, "grp", scatter_dimension=1, tiled=True)
    gate_sum, last_sum, first_half = lax.psum((gate_share, last_share, first_part), "grp")
    middle_sum, first_sum = lax.psum((middle_share, first_half), "seq")
    return gate_sum * factor, first_sum * factor, middle_sum * factor, last_sum * factor


PLANES = ("z", "y")


def dot(left, right):
    return jnp.dot(left, right, preferred_element_type=F32)


def dot_rows(left, right):
    return lax.dot_general(left, right, (((1,), (1,)), ((), ())), preferred_element_type=F32)


def exact(left, right):
    return jnp.dot(left, right, precision=lax.Precision.HIGHEST, preferred_element_type=F32)


def iota(shape, axis):
    return lax.broadcasted_iota(jnp.int32, shape, axis)


def place(size, block):
    source = ((iota((size, size), 0) // block) ^ lax.axis_index("z")) * block + iota((size, size), 0) % block
    return jnp.where(source == iota((size, size), 1), 1.0, 0.0)


def spread(factor, lanes, turned=False):
    size = factor.shape[0]
    wide = size * lanes
    tall = jnp.where(iota((wide, size), 0) // lanes == iota((wide, size), 1), 1.0, 0.0).astype(BF16)
    flat = jnp.where(iota((size, wide), 1) // lanes == iota((size, wide), 0), 1.0, 0.0).astype(BF16)
    picked = (dot_rows if turned else dot)(tall, factor).astype(BF16)
    same = iota((wide, wide), 0) % lanes == iota((wide, wide), 1) % lanes
    return jnp.where(same, dot(picked, flat), 0.0).astype(BF16)


def gather_diagonal(total, size, lanes):
    wide = size * lanes
    same = iota((wide, wide), 0) % lanes == iota((wide, wide), 1) % lanes
    kept = jnp.where(same, total, 0.0).reshape(size, lanes, wide).sum(axis=1)
    collect = jnp.where(iota((wide, size), 0) // lanes == iota((wide, size), 1), 1.0, 0.0)
    return exact(kept, collect)


def gate_of(rows, weight):
    return jax.nn.sigmoid(dot(rows, weight))


def open_kernel(planes, step_j, x_ref, g_ref, w_ref, a_ref, *refs):
    v_refs, wide = refs[:planes], refs[planes]
    n_i, _, lanes, width = x_ref.shape
    size, part = width // HEADS, n_i // planes

    @pl.when(pl.program_id(0) == 0)
    def _():
        moved = place(n_i, part).astype(BF16)
        for h in range(HEADS):
            wide[h] = spread(dot_rows(a_ref[h], moved).astype(BF16), lanes, turned=True)

    sent = []
    for j in range(step_j):
        rows = x_ref[:, j].reshape(n_i * lanes, width)
        up = g_ref[:, j].reshape(n_i * lanes, width).astype(F32)
        sent.append((up * gate_of(rows, w_ref[...])).astype(BF16))
    for h in range(HEADS):
        pair = jnp.concatenate([d[:, h * size : (h + 1) * size] for d in sent], axis=1)
        out = dot(wide[h], pair).astype(BF16)
        for m in range(planes):
            for j in range(step_j):
                piece = out[m * part * lanes : (m + 1) * part * lanes, j * size : (j + 1) * size]
                v_refs[m][:, j, :, h * size : (h + 1) * size] = piece.reshape(part, lanes, size)


def open_side(tokens, cotangent, gate_weight, first_factor, planes):
    n_i, n_j, lanes, width = tokens.shape
    step_j = 2
    block = pl.BlockSpec((n_i, step_j, lanes, width), lambda j: (0, j, 0, 0))
    part = pl.BlockSpec((n_i // planes, step_j, lanes, width), lambda j: (0, j, 0, 0))
    whole = lambda a: pl.BlockSpec(a.shape, lambda j: (0,) * a.ndim)
    count = tokens.size
    return pl.pallas_call(
        functools.partial(open_kernel, planes, step_j),
        grid=(n_j // step_j,),
        in_specs=[block, block, whole(gate_weight), whole(first_factor)],
        out_specs=[part] * planes,
        out_shape=[jax.ShapeDtypeStruct((n_i // planes, n_j, lanes, width), BF16)] * planes,
        scratch_shapes=[pltpu.VMEM((HEADS, n_i * lanes, n_i * lanes), BF16)],
        cost_estimate=pl.CostEstimate(
            flops=2 * count * (width + n_i * lanes), bytes_accessed=6 * count, transcendentals=count
        ),
        name="open_side",
    )(tokens, cotangent, gate_weight, first_factor)


def moved_last(factor, part):
    moved = place(factor.shape[0], part).astype(BF16)
    return dot_rows(dot(moved, factor).astype(BF16), moved).astype(BF16)


def forward_kernel(planes, b_ref, c_ref, *refs):
    x_refs, y_refs = refs[:planes], refs[planes : 2 * planes]
    bx_ref, wide = refs[2 * planes :]
    groups, pair_y, n_j, lanes, size = x_refs[0].shape
    part = pair_y * lanes
    last = moved_last(b_ref[0], part)
    wide[...] = spread(c_ref[0], lanes)

    def over_last(t, carry):
        g, j = t // (n_j // 2), (t % (n_j // 2)) * 2
        pair = [
            jnp.concatenate([ref[g, :, j + p].reshape(part, size) for ref in x_refs], axis=0) for p in range(2)
        ]
        out = dot(last, jnp.concatenate(pair, axis=1)).astype(BF16)
        for m in range(planes):
            for p in range(2):
                piece = out[m * part : (m + 1) * part, p * size : (p + 1) * size]
                bx_ref[m, g, :, j + p] = piece.reshape(pair_y, lanes, size)
        return carry

    lax.fori_loop(0, groups * n_j // 2, over_last, 0, unroll=2)
    for m in range(planes):
        held = [bx_ref[m, :, y].reshape(groups * n_j * lanes, size) for y in range(pair_y)]
        out = dot(wide[...], jnp.concatenate(held, axis=1)).astype(BF16)
        for y in range(pair_y):
            y_refs[m][:, y] = out[:, y * size : (y + 1) * size].reshape(groups, n_j, lanes, size)


def forward_side(values, last_factor, middle_factor):
    planes = len(values)
    groups, pair_y, n_j, lanes, width = values[0].shape
    size, n_middle = width // HEADS, groups * n_j
    block = pl.BlockSpec((groups, pair_y, n_j, lanes, size), lambda h: (0, 0, 0, 0, h))
    one = lambda a: pl.BlockSpec((1,) + a.shape[1:], lambda h: (h, 0, 0))
    count = values[0].size * planes
    shape = jax.ShapeDtypeStruct(values[0].shape, BF16)
    return pl.pallas_call(
        functools.partial(forward_kernel, planes),
        grid=(HEADS,),
        in_specs=[one(last_factor), one(middle_factor)] + [block] * planes,
        out_specs=[block] * planes
        + [pl.BlockSpec((planes, groups, pair_y, n_j, lanes, size), lambda h: (0, 0, 0, 0, 0, h))],
        out_shape=[shape] * planes + [jax.ShapeDtypeStruct((planes,) + values[0].shape, BF16)],
        scratch_shapes=[pltpu.VMEM((n_middle * lanes, n_middle * lanes), BF16)],
        cost_estimate=pl.CostEstimate(
            flops=2 * count * (n_middle * lanes + last_factor.shape[1]),
            bytes_accessed=6 * count,
            transcendentals=0,
        ),
        name="forward_side",
    )(last_factor, middle_factor, *values)


def backward_kernel(planes, b_ref, c_ref, bx_ref, *refs):
    x_refs, v_refs, u_refs = (refs[n * planes : (n + 1) * planes] for n in range(3))
    gl_ref, gm_ref, sent_all, cv, acc, wide = refs[3 * planes :]
    groups, pair_y, n_j, lanes, size = x_refs[0].shape
    rows, part = groups * n_j * lanes, pair_y * lanes
    wide[...] = spread(c_ref[0], lanes, turned=True)
    acc[...] = jnp.zeros_like(acc)
    for m in range(planes):
        sent_all[m] = v_refs[m][...]

    def over_middle(m, carry):
        sent = jnp.concatenate([sent_all[m, :, y].reshape(rows, size) for y in range(pair_y)], axis=1)
        held = jnp.concatenate([bx_ref[m, :, y].reshape(rows, size) for y in range(pair_y)], axis=1)
        acc[...] += dot_rows(sent, held)
        out = dot(wide[...], sent).astype(BF16)
        for y in range(pair_y):
            cv[m, :, y] = out[:, y * size : (y + 1) * size].reshape(groups, n_j, lanes, size)
        return carry

    lax.fori_loop(0, planes, over_middle, 0)
    gm_ref[0] = gather_diagonal(acc[...], groups * n_j, lanes)
    last = moved_last(b_ref[0], part)

    def over_last(t, total):
        g, j = t // (n_j // 2), (t % (n_j // 2)) * 2
        back, held = [
            jnp.concatenate(
                [
                    jnp.concatenate([ref[g, :, j + p].reshape(part, size) for ref in group], axis=0)
                    for p in range(2)
                ],
                axis=1,
            )
            for group in ([cv.at[m] for m in range(planes)], x_refs)
        ]
        out = dot(last, back).astype(BF16)
        for m in range(planes):
            for p in range(2):
                piece = out[m * part : (m + 1) * part, p * size : (p + 1) * size]
                u_refs[m][g, :, j + p] = piece.reshape(pair_y, lanes, size)
        return total + dot_rows(back, held)

    n_last = planes * part
    total = lax.fori_loop(0, groups * n_j // 2, over_last, jnp.zeros((n_last, n_last), F32), unroll=2)
    moved = place(n_last, part)
    gl_ref[0] = exact(exact(moved, total), moved)


def backward_side(sent, values, mixed, last_factor_t, middle_factor):
    planes = len(values)
    groups, pair_y, n_j, lanes, width = values[0].shape
    size, n_middle, n_last = width // HEADS, groups * n_j, last_factor_t.shape[1]
    block = pl.BlockSpec((groups, pair_y, n_j, lanes, size), lambda h: (0, 0, 0, 0, h))
    every = (planes, groups, pair_y, n_j, lanes, size)
    one = lambda n: pl.BlockSpec((1, n, n), lambda h: (h, 0, 0))
    count = values[0].size * planes
    wide = n_middle * lanes
    return pl.pallas_call(
        functools.partial(backward_kernel, planes),
        grid=(HEADS,),
        in_specs=[one(n_last), one(n_middle), pl.BlockSpec(every, lambda h: (0, 0, 0, 0, 0, h))]
        + [block] * (2 * planes),
        out_specs=[block] * planes + [one(n_last), one(n_middle)],
        out_shape=[jax.ShapeDtypeStruct(values[0].shape, BF16)] * planes
        + [
            jax.ShapeDtypeStruct((HEADS, n_last, n_last), F32),
            jax.ShapeDtypeStruct((HEADS, n_middle, n_middle), F32),
        ],
        scratch_shapes=[
            pltpu.VMEM(every, BF16),
            pltpu.VMEM(every, BF16),
            pltpu.VMEM((wide, wide), F32),
            pltpu.VMEM((wide, wide), BF16),
        ],
        cost_estimate=pl.CostEstimate(
            flops=4 * count * (wide + n_last), bytes_accessed=8 * count, transcendentals=0
        ),
        name="backward_side",
    )(last_factor_t, middle_factor, mixed, *values, *sent)


def close_kernel(planes, step_j, x_ref, g_ref, w_ref, a_ref, *refs):
    y_refs = refs[:planes]
    t_ref, gg_ref, gf_ref, acc, wide = refs[planes:]
    n_i, _, lanes, width = x_ref.shape
    size, rows_n = width // HEADS, n_i * lanes
    part = n_i // planes

    @pl.when(pl.program_id(0) == 0)
    def _():
        acc[...] = jnp.zeros_like(acc)
        gg_ref[...] = jnp.zeros_like(gg_ref)
        moved = place(n_i, part).astype(BF16)
        for h in range(HEADS):
            wide[h] = spread(dot_rows(a_ref[h], moved).astype(BF16), lanes)

    rows, ups, gates, mixes, sent = [], [], [], [], []
    for j in range(step_j):
        rows.append(x_ref[:, j].reshape(rows_n, width))
        ups.append(g_ref[:, j].reshape(rows_n, width).astype(F32))
        gates.append(gate_of(rows[j], w_ref[...]))
        mixes.append(jnp.concatenate([ref[:, j].reshape(part * lanes, width) for ref in y_refs], axis=0))
        sent.append((ups[j] * gates[j]).astype(BF16))
    outs = []
    for h in range(HEADS):
        cut = slice(h * size, (h + 1) * size)
        held = jnp.concatenate([m[:, cut] for m in mixes], axis=1)
        back = jnp.concatenate([d[:, cut] for d in sent], axis=1)
        acc[h] += dot_rows(back, held)
        outs.append(dot(wide[h], held).astype(BF16).astype(F32))
    for j in range(step_j):
        mixer = jnp.concatenate([o[:, j * size : (j + 1) * size] for o in outs], axis=1)
        d_pre = (ups[j] * mixer * gates[j] * (1.0 - gates[j])).astype(BF16)
        t_ref[:, j] = dot_rows(d_pre, w_ref[...]).astype(BF16).reshape(n_i, lanes, width)
        gg_ref[...] += lax.dot_general(
            rows[j], d_pre, (((0,), (0,)), ((), ())), preferred_element_type=F32
        )

    @pl.when(pl.program_id(0) == pl.num_programs(0) - 1)
    def _():
        for h in range(HEADS):
            gf_ref[h] = exact(gather_diagonal(acc[h], n_i, lanes), place(n_i, part))


def close_side(tokens, cotangent, mixed, gate_weight, first_factor):
    planes = len(mixed)
    n_i, n_j, lanes, width = tokens.shape
    step_j = 2
    block = pl.BlockSpec((n_i, step_j, lanes, width), lambda j: (0, j, 0, 0))
    part = pl.BlockSpec((n_i // planes, step_j, lanes, width), lambda j: (0, j, 0, 0))
    whole = lambda shape: pl.BlockSpec(shape, lambda j: (0,) * len(shape))
    count = tokens.size
    return pl.pallas_call(
        functools.partial(close_kernel, planes, step_j),
        grid=(n_j // step_j,),
        in_specs=[block, block, whole(gate_weight.shape), whole(first_factor.shape)] + [part] * planes,
        out_specs=[block, whole((width, width)), whole((HEADS, n_i, n_i))],
        out_shape=[
            jax.ShapeDtypeStruct(tokens.shape, BF16),
            jax.ShapeDtypeStruct((width, width), F32),
            jax.ShapeDtypeStruct((HEADS, n_i, n_i), F32),
        ],
        scratch_shapes=[
            pltpu.VMEM((HEADS, n_i * lanes, n_i * lanes), F32),
            pltpu.VMEM((HEADS, n_i * lanes, n_i * lanes), BF16),
        ],
        cost_estimate=pl.CostEstimate(
            flops=2 * count * (3 * width + 2 * n_i * lanes),
            bytes_accessed=8 * count,
            transcendentals=count,
        ),
        name="close_side",
    )(tokens, cotangent, gate_weight, first_factor, *mixed)


def finish_kernel(z_ref, b_ref, t_ref, *refs):
    refs[-1][...] = (b_ref[...].astype(F32) + t_ref[...].astype(F32)).astype(BF16)


def finish(back, gate_term, m, held=None):
    part, n_j, lanes, width = back.shape
    step = part // 4
    here = pl.BlockSpec((step, n_j, lanes, width), lambda t, z: (t, 0, 0, 0))
    there = pl.BlockSpec((step, n_j, lanes, width), lambda t, z: ((z[0] ^ m) * 4 + t, 0, 0, 0))
    more = [] if held is None else [held]
    return pl.pallas_call(
        finish_kernel,
        grid_spec=pltpu.PrefetchScalarGridSpec(
            num_scalar_prefetch=1,
            grid=(4,),
            in_specs=[here, there] + [pl.BlockSpec(memory_space=pl.ANY)] * len(more),
            out_specs=there,
        ),
        out_shape=jax.ShapeDtypeStruct(gate_term.shape, BF16),
        input_output_aliases={3: 0} if more else {},
        cost_estimate=pl.CostEstimate(flops=back.size, bytes_accessed=6 * back.size, transcendentals=0),
    )(lax.axis_index("z").reshape(1), back, gate_term, *more)


def over_z(part, m):
    if m == 0:
        return part
    pairs = [(z, z ^ m) for z in range(lax.axis_size("z"))]
    return lax.ppermute(part, "z", pairs)


def in_plane(part):
    return lax.all_to_all(part, ("grp", "y"), split_axis=0, concat_axis=0, tiled=True)


def shifted(parts, axis):
    count = lax.axis_size(axis)
    me = lax.axis_index(axis)
    out = []
    for d in range(1, count):
        part = lax.dynamic_index_in_dim(parts, (me + d) % count, 0, False)
        out.append(lax.ppermute(part, axis, [(i, (i + d) % count) for i in range(count)]))
    return out


def share_kernel(factor, *refs):
    total = refs[0][...]
    for part in refs[1:-1]:
        total += part[...]
    refs[-1][...] = total * factor


def share_sum(parts, factor):
    return pl.pallas_call(
        functools.partial(share_kernel, factor),
        out_shape=jax.ShapeDtypeStruct(parts[0].shape, F32),
        name="share_sum",
    )(*parts)


def ordered_kernel(axis, *refs):
    parts, out_ref, held = refs[:-2], refs[-2], refs[-1]
    count = len(parts)
    me = lax.axis_index(axis)
    for d, part in enumerate(parts):
        held[d] = part[...]
    total = held[lax.rem(me + count, count)]
    for source in range(1, count):
        total += held[lax.rem(me - source + count, count)]
    out_ref[...] = total


def ordered_sum(parts, axis):
    shape = parts[0].shape
    return pl.pallas_call(
        functools.partial(ordered_kernel, axis),
        out_shape=jax.ShapeDtypeStruct(shape, F32),
        scratch_shapes=[pltpu.VMEM((len(parts),) + shape, F32)],
        name="ordered_sum",
    )(*parts)


def reduced_direct(gate_part, first_part, middle_part, last_part, factor):
    groups, blocks = lax.axis_size("grp"), lax.axis_size(PLANES)
    width = gate_part.shape[0]
    n_last, n_middle, n_first = last_part.shape[1], middle_part.shape[1], first_part.shape[1]
    lane = width // groups
    own = HEADS // groups

    def flat(parts):
        return parts.reshape(parts.shape[0], -1, lane)

    packed = jnp.concatenate(
        [
            gate_part.reshape(width, groups, lane).transpose(1, 0, 2),
            flat(last_part.reshape(groups, -1)),
            flat(middle_part.reshape(HEADS, groups, -1).transpose(1, 0, 2)),
            flat(first_part.reshape(groups, -1)),
        ],
        axis=1,
    )
    mine = lax.dynamic_index_in_dim(packed, lax.axis_index("grp"), 0, False)
    share = share_sum([mine] + shifted(packed, "grp"), factor)
    cuts = [width, own * n_last * n_last // lane, HEADS * n_middle * n_middle // groups // lane]
    gate, last, middle, first = jnp.split(share, [sum(cuts[: n + 1]) for n in range(3)])
    last = last.reshape(own, blocks, n_last // blocks, n_last).transpose(1, 0, 2, 3)
    again = jnp.concatenate(
        [
            gate.reshape(blocks, -1, lane),
            flat(last.reshape(blocks, -1)),
            jnp.broadcast_to(middle, (blocks,) + middle.shape),
            jnp.broadcast_to(first, (blocks,) + first.shape),
        ],
        axis=1,
    )
    mine = lax.dynamic_index_in_dim(again, lax.axis_index(PLANES), 0, False)
    total = ordered_sum([mine] + shifted(again, PLANES), PLANES)
    cuts = [width // blocks, own * n_last * n_last // blocks // lane, middle.shape[0]]
    gate, last, middle, first = jnp.split(total, [sum(cuts[: n + 1]) for n in range(3)])
    give = jnp.concatenate([gate, last, first])
    me = lax.axis_index("grp")
    spread_out = jnp.zeros((groups,) + give.shape, F32)
    spread_out = lax.dynamic_update_index_in_dim(spread_out, give, me, 0)
    for d, part in enumerate(shifted(jnp.broadcast_to(give, (groups,) + give.shape), "grp"), 1):
        spread_out = lax.dynamic_update_index_in_dim(spread_out, part, (me - d) % groups, 0)
    gate, last, first = jnp.split(spread_out, [gate.shape[0], gate.shape[0] + last.shape[0]], axis=1)
    return (
        gate.transpose(1, 0, 2).reshape(-1, width),
        first.reshape(HEADS, n_first, n_first),
        middle.reshape(HEADS, n_middle // groups, n_middle),
        last.reshape(HEADS, n_last // blocks, n_last),
    )


def ordered(tokens, cotangent, gate_weight, first_factor, middle_factor, last_factor):
    groups, planes, pair_y = (lax.axis_size(axis) for axis in ("grp", "z", "y"))
    part = tokens.shape[0] // planes
    split = (groups, pair_y) + tokens.shape[1:]
    home = (part,) + tokens.shape[1:]
    z = lax.axis_index("z")
    held = [lax.dynamic_slice_in_dim(tokens, (z ^ m) * part, part, 0) for m in range(planes)]
    at_whole = [in_plane(over_z(held[m], m)).reshape(split) for m in range(planes)]
    sent = open_side(tokens, cotangent, gate_weight, first_factor, planes)
    sent_whole = [over_z(in_plane(sent[m]), m).reshape(split) for m in range(planes)]
    *forward, mixed = forward_side(at_whole, last_factor, middle_factor)
    forward_home = [over_z(in_plane(forward[m].reshape(home)), m) for m in range(planes)]
    *backward, last_part, middle_part = backward_side(
        sent_whole, at_whole, mixed, last_factor.transpose(0, 2, 1), middle_factor
    )
    back_home = [over_z(in_plane(backward[m].reshape(home)), m) for m in range(planes)]
    gate_term, gate_part, first_part = close_side(
        tokens, cotangent, forward_home, gate_weight, first_factor
    )
    sums = reduced_direct(
        gate_part, first_part, middle_part, last_part, 1.0 / math.sqrt(positions(tokens, PLANES))
    )
    d_tokens = None
    for m in range(planes):
        d_tokens = finish(back_home[m], gate_term, m, d_tokens)
    return (d_tokens,) + sums


def direct(*arrays):
    return ordered(*arrays)


def fits(shape, groups, blocks):
    n_i, n_j, lanes, width = shape
    planes = blocks // 2
    return (
        n_i == groups * blocks
        and blocks == 2 * planes
        and planes & (planes - 1) == 0
        and n_i % (4 * planes) == 0
        and lanes % 16 == 0
        and n_j % 2 == 0
        and width == groups * 128
        and HEADS % groups == 0
        and width % (HEADS * 128) == 0
    )


def shards_of(mesh, tokens):
    groups, blocks = mesh.shape["grp"], mesh.shape["seq"]
    n_i, n_j, n_k, width = tokens.shape
    if fits((n_i, n_j // groups, n_k // blocks, width), groups, blocks):
        devices = mesh.devices.reshape(groups, blocks // 2, 2)
        return direct, jax.sharding.Mesh(devices, ("grp",) + PLANES), PLANES
    return general, mesh, "seq"


def solution(mesh):
    def step(*arrays):
        body, fine, seq = shards_of(mesh, arrays[0])
        spread_in = P(None, "grp", seq, None)
        in_specs = (spread_in, spread_in, P(), P(), P(), P())
        out_specs = (spread_in, P(seq, None), P(), P(None, "grp", None), P(None, seq, None))
        return jax.shard_map(body, mesh=fine, in_specs=in_specs, out_specs=out_specs, check_vma=False)(*arrays)

    return step
```

time: 897 us -> 1080 us (1.20)
  waiting for transfers between devices: 350 us -> 529 us
  starting transfers between devices: 30.3 us -> 203 us
  blocking collectives: 331 us -> 176 us
  Pallas kernels: 168 us -> 149 us
    ppermute x0 -> x12, waiting for transfers between devices: none -> 424 us  [over_z(): return lax.ppermute(part, 'z', pairs)]
    all_to_all x3 -> x10, waiting for transfers between devices: 331 us -> 88.8 us  [in_plane(): lax.all_to_all(part, ('grp', 'y'), split_axis=0, concat_axis=0, tiled=True)]
    all_to_all x2 -> x6, blocking collectives: 331 us -> 176 us  [in_plane(): lax.all_to_all(part, ('grp', 'y'), split_axis=0, concat_axis=0, tiled=True)]
    ppermute x0 -> x12, starting transfers between devices: none -> 97.9 us  [over_z(): return lax.ppermute(part, 'z', pairs)]
    ppermute x13, starting transfers between devices: 16.2 us -> 61.6 us  [shifted(): lax.ppermute(part, axis, [(i, (i + d) % count) for i in range(count)])]
    all_to_all x3 -> x10, starting transfers between devices: 14.1 us -> 43.9 us  [in_plane(): lax.all_to_all(part, ('grp', 'y'), split_axis=0, concat_axis=0, tiled=True)]
    pallas_call x6 -> x8, Pallas kernels: 164 us -> 145 us  [the longest x1 50.8 us: backward_side(): pl.pallas_call(functools.partial(backward_kernel, planes), grid=(HEADS,),...]
  transfers between devices with their start and end apart: 16 -> 35, of which waited for: 6 -> 17; matrix products, arithmetic and copies ran while one was open for 1% -> 1% of each run, Pallas kernels for 11% -> 9%
where the time goes in v3:
time: 1080 us
  waiting for transfers between devices  529 us (49%)
  starting transfers between devices  203 us (19%)
  blocking collectives  176 us (16%)
  Pallas kernels  149 us (14%)
  local copies, waits for them, and re-layouts  22.9 us (2%)
    ppermute x12, waiting for transfers between devices, over_z(): return lax.ppermute(part, 'z', pairs)  424 us
    all_to_all x6, blocking collectives, in_plane(): lax.all_to_all(part, ('grp', 'y'), split_axis=0, concat_axis=0, tiled=True)  176 us
    ppermute x12, starting transfers between devices, over_z(): return lax.ppermute(part, 'z', pairs)  97.9 us
    all_to_all x10, waiting for transfers between devices, in_plane(): lax.all_to_all(part, ('grp', 'y'), split_axis=0, concat_axis=0, tiled=True)  88.8 us
    ppermute x13, starting transfers between devices, shifted(): lax.ppermute(part, axis, [(i, (i + d) % count) for i in range(count)])  61.6 us
    pallas_call x1, Pallas kernels, backward_side(): pl.pallas_call(functools.partial(backward_kernel, planes), grid=(HEADS,),...  50.8 us
    all_to_all x10, starting transfers between devices, in_plane(): lax.all_to_all(part, ('grp', 'y'), split_axis=0, concat_axis=0, tiled=True)  43.9 us
    pallas_call x1, Pallas kernels, close_side(): pl.pallas_call(functools.partial(close_kernel, planes, step_j), grid=(n_j...  31.5 us
  transfers between devices with their start and end apart: 35, of which 17 were waited for; matrix products, arithmetic and copies ran while one was open for 1% of the time, Pallas kernels for 9%

profile of v3, /device:TPU:0, one launch (start us, length us, event | category | flops | bytes accessed | tf_op | source)
XLA Modules:
  0.0 1080.9 jit_solution(2428432019548169174)
XLA Ops:
  0.7 6.7 constant_dynamic-slice_fusion
  7.4 5.2 all-to-all-start
  12.6 17.4 %open_side.1 = (bf16[8,16,16,512]{3,2,1,0:T(8,128)(2,1)}, bf16[8,16,16,512]{3,2,1,0:T(8,128)(2,1)}, bf16[8,16,16,512]{3,2,1,0:T(8,128)(2,1)}, bf16[8,16,16,512]{3,2,1,0:T(8,128)(2,1)}) custom-call(bf16[32,16,16,512]{3,2,1,0:T(8,128)(2,1)} %x_ref.3, bf16[32,16,16,512]{3,2,1,0:T(8,128)(2,1)} %g_ref.3, bf16[512,512]{1,0:T(8,128)(2,1)} %w_ref.3, ...), custom_call_target="tpu_custom_call" | custom-call | flops 8589934592 | bytes 25165824 | tf_op jit(solution)/shard_map/open_side/pallas_call | solution.py:169
  30.0 8.4 all-to-all-done
  38.4 30.0 %all_to_all.80 = bf16[8,16,16,512]{3,2,1,0:T(8,128)(2,1)} all-to-all(bf16[8,16,16,512]{3,2,1,0:T(8,128)(2,1)} %get-tuple-element.25), channel_id=1, replica_groups=mesh['grp'=4,'z'=4,'y'=2] {'grp','y'}, dimensions={0} | all-to-all | bytes 4194304 | tf_op jit(solution)/shard_map/all_to_all | solution.py:428
  75.0 23.6 %all-to-all-done.6 = bf16[8,16,16,512]{3,2,1,0:T(8,128)(2,1)} async-done(((bf16[8,16,16,512]{3,2,1,0:T(8,128)(2,1)}), bf16[8,16,16,512]{3,2,1,0:T(8,128)(2,1)}, u32[]{:S(2)}, u32[]{:S(2)}) %all-to-all-start.6) | async-done | bytes 2097184 | tf_op jit(solution)/shard_map/all_to_all | solution.py:428
  106.1 22.6 %all-to-all-done.7 = bf16[8,16,16,512]{3,2,1,0:T(8,128)(2,1)} async-done(((bf16[8,16,16,512]{3,2,1,0:T(8,128)(2,1)}), bf16[8,16,16,512]{3,2,1,0:T(8,128)(2,1)}, u32[]{:S(2)}, u32[]{:S(2)}) %all-to-all-start.7) | async-done | bytes 2097184 | tf_op jit(solution)/shard_map/all_to_all | solution.py:428
  128.7 8.8 collective-permute-done
  143.4 99.5 %collective-permute-done.1 = bf16[8,16,16,512]{3,2,1,0:T(8,128)(2,1)} collective-permute-done((bf16[8,16,16,512]{3,2,1,0:T(8,128)(2,1)}, bf16[8,16,16,512]{3,2,1,0:T(8,128)(2,1)}, u32[]{:S(2)}, u32[]{:S(2)}) %collective-permute-start.1) | collective-permute-done | bytes 2097184 | tf_op jit(solution)/shard_map/ppermute | solution.py:424
  247.2 25.7 %all-to-all-done.2 = bf16[8,16,16,512]{3,2,1,0:T(8,128)(2,1)} async-done(((bf16[8,16,16,512]{3,2,1,0:T(8,128)(2,1)}), bf16[8,16,16,512]{3,2,1,0:T(8,128)(2,1)}, u32[]{:S(2)}, u32[]{:S(2)}) %all-to-all-start.2) | async-done | bytes 2097184 | tf_op jit(solution)/shard_map/all_to_all | solution.py:428
  277.3 15.4 %collective-permute-start.3 = (bf16[8,16,16,512]{3,2,1,0:T(8,128)(2,1)S(1)}, bf16[8,16,16,512]{3,2,1,0:T(8,128)(2,1)}, u32[]{:S(2)}, u32[]{:S(2)}) collective-permute-start(bf16[8,16,16,512]{3,2,1,0:T(8,128)(2,1)S(1)} %copy-done.2), channel_id=1, source_target_pairs={{0,2},{2,0},{4,6},{6,4},{1,3},{3,1},{5,7},{7,5},{8,10},{10,8},{12,... | collective-permute-start | bytes 6291464 | tf_op jit(solution)/shard_map/ppermute | solution.py:424
  296.2 6.9 all-to-all-done.3
  303.1 4.7 all-to-all-start.4
  308.5 28.3 %forward_side.1 = (bf16[4,2,16,16,512]{4,3,2,1,0:T(8,128)(2,1)}, bf16[4,2,16,16,512]{4,3,2,1,0:T(8,128)(2,1)}, bf16[4,2,16,16,512]{4,3,2,1,0:T(8,128)(2,1)}, bf1...) custom-call(bf16[4,128,128]{2,1,0:T(8,128)(2,1)} %b_ref.1, bf16[4,64,64]{2,1,0:T(8,128)(2,1)} %c_ref.3, ...), custom_call_target="tpu_custom_call" | custom-call | flops 9663676416 | bytes 25165824 | tf_op jit(solution)/shard_map/forward_side/pallas_call | solution.py:224
  336.8 46.9 %collective-permute-done.3 = bf16[8,16,16,512]{3,2,1,0:T(8,128)(2,1)} collective-permute-done((bf16[8,16,16,512]{3,2,1,0:T(8,128)(2,1)S(1)}, bf16[8,16,16,512]{3,2,1,0:T(8,128)(2,1)}, u32[]{:S(2)}, u32[]{:S(2)}) %collective-permute-start.3) | collective-permute-done | bytes 2097184 | tf_op jit(solution)/shard_map/ppermute | solution.py:424
  383.7 48.6 %collective-permute-done.4 = bf16[8,16,16,512]{3,2,1,0:T(8,128)(2,1)} collective-permute-done((bf16[8,16,16,512]{3,2,1,0:T(8,128)(2,1)}, bf16[8,16,16,512]{3,2,1,0:T(8,128)(2,1)}, u32[]{:S(2)}, u32[]{:S(2)}) %collective-permute-start.4) | collective-permute-done | bytes 2097184 | tf_op jit(solution)/shard_map/ppermute | solution.py:424
  432.3 50.8 %backward_side.1 = (bf16[4,2,16,16,512]{4,3,2,1,0:T(8,128)(2,1)}, bf16[4,2,16,16,512]{4,3,2,1,0:T(8,128)(2,1)}, bf16[4,2,16,16,512]{4,3,2,1,0:T(8,128)(2,1)}, bf...) custom-call(bf16[4,128,128]{2,1,0:T(8,128)(2,1)} %bitcast.76, ...), custom_call_target="tpu_custom_call" | custom-call | flops 19327352832 | bytes 33554432 | tf_op jit(solution)/shard_map/backward_side/pallas_call | solution.py:298
  483.2 30.1 %all_to_all.81 = bf16[8,16,16,512]{3,2,1,0:T(8,128)(2,1)} all-to-all(bf16[8,16,16,512]{3,2,1,0:T(8,128)(2,1)} %bitcast.72), channel_id=1, replica_groups=mesh['grp'=4,'z'=4,'y'=2] {'grp','y'}, dimensions={0} | all-to-all | bytes 4194304 | tf_op jit(solution)/shard_map/all_to_all | solution.py:428
  513.3 29.0 %all_to_all.82.refs_0_ = bf16[8,16,16,512]{3,2,1,0:T(8,128)(2,1)} all-to-all(bf16[8,16,16,512]{3,2,1,0:T(8,128)(2,1)S(1)} %bitcast.71), channel_id=1, replica_groups=mesh['grp'=4,'z'=4,'y'=2] {'grp','y'}, dimensions={0} | all-to-all | bytes 4194304 | tf_op jit(solution)/shard_map/all_to_all | solution.py:428
  542.3 29.0 %all_to_all.83 = bf16[8,16,16,512]{3,2,1,0:T(8,128)(2,1)} all-to-all(bf16[8,16,16,512]{3,2,1,0:T(8,128)(2,1)S(1)} %bitcast.70), channel_id=1, replica_groups=mesh['grp'=4,'z'=4,'y'=2] {'grp','y'}, dimensions={0} | all-to-all | bytes 4194304 | tf_op jit(solution)/shard_map/all_to_all | solution.py:428
  571.2 28.9 %all_to_all.84 = bf16[8,16,16,512]{3,2,1,0:T(8,128)(2,1)} all-to-all(bf16[8,16,16,512]{3,2,1,0:T(8,128)(2,1)S(1)} %bitcast.69), channel_id=1, replica_groups=mesh['grp'=4,'z'=4,'y'=2] {'grp','y'}, dimensions={0} | all-to-all | bytes 4194304 | tf_op jit(solution)/shard_map/all_to_all | solution.py:428
  600.2 28.8 %all_to_all.85 = bf16[8,16,16,512]{3,2,1,0:T(8,128)(2,1)} all-to-all(bf16[8,16,16,512]{3,2,1,0:T(8,128)(2,1)S(1)} %bitcast.68), channel_id=1, replica_groups=mesh['grp'=4,'z'=4,'y'=2] {'grp','y'}, dimensions={0} | all-to-all | bytes 4194304 | tf_op jit(solution)/shard_map/all_to_all | solution.py:428
  633.4 44.7 %collective-permute-start.7 = (bf16[8,16,16,512]{3,2,1,0:T(8,128)(2,1)}, bf16[8,16,16,512]{3,2,1,0:T(8,128)(2,1)}, u32[]{:S(2)}, u32[]{:S(2)}) collective-permute-start(bf16[8,16,16,512]{3,2,1,0:T(8,128)(2,1)} %all_to_all.83), channel_id=1, source_target_pairs={{0,2},{2,0},{4,6},{6,4},{1,3},{3,1},{5,7},{7,5},{8,10},{10,8},{12,... | collective-permute-start | bytes 6291464 | tf_op jit(solution)/shard_map/ppermute | solution.py:424
  688.3 21.6 %collective-permute-start.10 = (bf16[8,16,16,512]{3,2,1,0:T(8,128)(2,1)}, bf16[8,16,16,512]{3,2,1,0:T(8,128)(2,1)}, u32[]{:S(2)}, u32[]{:S(2)}) collective-permute-start(bf16[8,16,16,512]{3,2,1,0:T(8,128)(2,1)} %all-to-all-done.13), channel_id=1, source_target_pairs={{0,4},{2,6},{4,0},{6,2},{1,5},{3,7},{5,1},{7,3},{8,12},{10,14},{12... | collective-permute-start | bytes 6291464 | tf_op jit(solution)/shard_map/ppermute | solution.py:424
  716.6 52.8 %collective-permute-done.7.refs_1_ = bf16[8,16,16,512]{3,2,1,0:T(8,128)(2,1)} collective-permute-done((bf16[8,16,16,512]{3,2,1,0:T(8,128)(2,1)}, bf16[8,16,16,512]{3,2,1,0:T(8,128)(2,1)}, u32[]{:S(2)}, u32[]{:S(2)}) %collective-permute-start.7) | collective-permute-done | bytes 2097184 | tf_op jit(solution)/shard_map/ppermute | solution.py:424
  769.4 137.8 %collective-permute-done.8.refs_2_ = bf16[8,16,16,512]{3,2,1,0:T(8,128)(2,1)} collective-permute-done((bf16[8,16,16,512]{3,2,1,0:T(8,128)(2,1)}, bf16[8,16,16,512]{3,2,1,0:T(8,128)(2,1)}, u32[]{:S(2)}, u32[]{:S(2)}) %collective-permute-start.8) | collective-permute-done | bytes 2097184 | tf_op jit(solution)/shard_map/ppermute | solution.py:424
  907.2 31.5 %close_side.1 = (bf16[32,16,16,512]{3,2,1,0:T(8,128)(2,1)}, f32[512,512]{1,0:T(8,128)}, f32[4,32,32]{2,1,0:T(8,128)}) custom-call(bf16[32,16,16,512]{3,2,1,0:T(8,128)(2,1)} %x_ref.3, bf16[32,16,16,512]{3,2,1,0:T(8,128)(2,1)} %g_ref.3, bf16[512,512]{1,0:T(8,128)(2,1)} %w_ref.3, bf16[4,32,32]{2,1,0:T(8,128)(2,1)} %a_ref.3, ...), custom_call_target="tpu_custom_call" | custom-call | flops 21474836480 | bytes 33554432 | tf_op jit(solution)/shard_map/close_side/pallas_call | solution.py:373
  943.7 8.1 collective-permute-done.12.refs_1_
  953.0 6.2 collective-permute-done.14.refs_3_
  966.7 46.0 %collective-permute-start.16 = (f32[120,128]{1,0:T(8,128)S(1)}, f32[120,128]{1,0:T(8,128)S(1)}, u32[]{:S(2)}, u32[]{:S(2)}) collective-permute-start(f32[120,128]{1,0:T(8,128)S(1)} %get-tuple-element.54), channel_id=1, source_target_pairs={{0,2},{1,3},{2,4},{3,5},{4,6},{5,7},{6,0},{7,1},{8,10},{9,11},{10,... | collective-permute-start | bytes 184328 | tf_op jit(solution)/shard_map/ppermute | solution.py:437
  1014.6 29.6 %collective-permute-done.10.b_ref = bf16[8,16,16,512]{3,2,1,0:T(8,128)(2,1)} collective-permute-done((bf16[8,16,16,512]{3,2,1,0:T(8,128)(2,1)}, bf16[8,16,16,512]{3,2,1,0:T(8,128)(2,1)}, u32[]{:S(2)}, u32[]{:S(2)}) %collective-permute-start.10) | collective-permute-done | bytes 2097184 | tf_op jit(solution)/shard_map/ppermute | solution.py:424
  1044.2 6.0 collective-permute-start.19
  (123 shorter events, 100.2 us)
Async XLA Ops:
  7.4 31.1 %all-to-all-start = ((bf16[8,16,16,512]{3,2,1,0:T(8,128)(2,1)}), bf16[8,16,16,512]{3,2,1,0:T(8,128)(2,1)}, u32[]{:S(2)}, u32[]{:S(2)}) async-start(bf16[8,16,16,512]{3,2,1,0:T(8,128)(2,1)} %get-tuple-element.44), calls=%async_computation | async-start | bytes 4194304 | tf_op jit(solution)/shard_map/all_to_all | solution.py:428
  68.4 30.1 %all-to-all-start.6 = ((bf16[8,16,16,512]{3,2,1,0:T(8,128)(2,1)}), bf16[8,16,16,512]{3,2,1,0:T(8,128)(2,1)}, u32[]{:S(2)}, u32[]{:S(2)}) async-start(bf16[8,16,16,512]{3,2,1,0:T(8,128)(2,1)} %get-tuple-element.26), calls=%async_computation.6 | async-start | bytes 4194304 | tf_op jit(solution)/shard_map/all_to_all | solution.py:428
  72.8 64.7 %collective-permute-start = (bf16[8,16,16,512]{3,2,1,0:T(8,128)(2,1)}, bf16[8,16,16,512]{3,2,1,0:T(8,128)(2,1)}, u32[]{:S(2)}, u32[]{:S(2)}) collective-permute-start(bf16[8,16,16,512]{3,2,1,0:T(8,128)(2,1)} %get-tuple-element.43), channel_id=1, source_target_pairs={{0,2},{2,0},{4,6},{6,4},{1,3},{3,1},{5,7},{7,5},{8,10},{10,8},{12,... | collective-permute-start | bytes 6291464 | tf_op jit(solution)/shard_map/ppermute | solution.py:424
  98.6 30.1 %all-to-all-start.7 = ((bf16[8,16,16,512]{3,2,1,0:T(8,128)(2,1)}), bf16[8,16,16,512]{3,2,1,0:T(8,128)(2,1)}, u32[]{:S(2)}, u32[]{:S(2)}) async-start(bf16[8,16,16,512]{3,2,1,0:T(8,128)(2,1)} %get-tuple-element.27), calls=%async_computation.7 | async-start | bytes 4194304 | tf_op jit(solution)/shard_map/all_to_all | solution.py:428
  102.9 139.9 %collective-permute-start.1 = (bf16[8,16,16,512]{3,2,1,0:T(8,128)(2,1)}, bf16[8,16,16,512]{3,2,1,0:T(8,128)(2,1)}, u32[]{:S(2)}, u32[]{:S(2)}) collective-permute-start(bf16[8,16,16,512]{3,2,1,0:T(8,128)(2,1)} %get-tuple-element.42), channel_id=1, source_target_pairs={{0,4},{2,6},{4,0},{6,2},{1,5},{3,7},{5,1},{7,3},{8,12},{10,14},{12... | collective-permute-start | bytes 6291464 | tf_op jit(solution)/shard_map/ppermute | solution.py:424
  137.5 105.4 %all-to-all-start.1 = ((bf16[8,16,16,512]{3,2,1,0:T(8,128)(2,1)}), bf16[8,16,16,512]{3,2,1,0:T(8,128)(2,1)}, u32[]{:S(2)}, u32[]{:S(2)}) async-start(bf16[8,16,16,512]{3,2,1,0:T(8,128)(2,1)} %collective-permute-done), calls=%async_computation.1 | async-start | bytes 4194304 | tf_op jit(solution)/shard_map/all_to_all | solution.py:428
  141.8 105.4 %collective-permute-start.2 = (bf16[8,16,16,512]{3,2,1,0:T(8,128)(2,1)S(1)}, bf16[8,16,16,512]{3,2,1,0:T(8,128)(2,1)}, u32[]{:S(2)}, u32[]{:S(2)}) collective-permute-start(bf16[8,16,16,512]{3,2,1,0:T(8,128)(2,1)S(1)} %get-tuple-element.41), channel_id=1, source_target_pairs={{0,6},{2,4},{4,2},{6,0},{1,7},{3,5},{5,3},{7,1},{8,14},{10,12},{12... | collective-permute-start | bytes 6291464 | tf_op jit(solution)/shard_map/ppermute | solution.py:424
  242.8 30.1 %all-to-all-start.2 = ((bf16[8,16,16,512]{3,2,1,0:T(8,128)(2,1)}), bf16[8,16,16,512]{3,2,1,0:T(8,128)(2,1)}, u32[]{:S(2)}, u32[]{:S(2)}) async-start(bf16[8,16,16,512]{3,2,1,0:T(8,128)(2,1)} %collective-permute-done.1), calls=%async_computation.2 | async-start | bytes 4194304 | tf_op jit(solution)/shard_map/all_to_all | solution.py:428
  273.0 30.1 %all-to-all-start.3 = ((bf16[8,16,16,512]{3,2,1,0:T(8,128)(2,1)}), bf16[8,16,16,512]{3,2,1,0:T(8,128)(2,1)}, u32[]{:S(2)}, u32[]{:S(2)}) async-start(bf16[8,16,16,512]{3,2,1,0:T(8,128)(2,1)} %collective-permute-done.2), calls=%async_computation.3 | async-start | bytes 4194304 | tf_op jit(solution)/shard_map/all_to_all | solution.py:428
  277.3 106.4 %collective-permute-start.3 = (bf16[8,16,16,512]{3,2,1,0:T(8,128)(2,1)S(1)}, bf16[8,16,16,512]{3,2,1,0:T(8,128)(2,1)}, u32[]{:S(2)}, u32[]{:S(2)}) collective-permute-start(bf16[8,16,16,512]{3,2,1,0:T(8,128)(2,1)S(1)} %copy-done.2), channel_id=1, source_target_pairs={{0,2},{2,0},{4,6},{6,4},{1,3},{3,1},{5,7},{7,5},{8,10},{10,8},{12,... | collective-permute-start | bytes 6291464 | tf_op jit(solution)/shard_map/ppermute | solution.py:424
  292.7 139.6 %collective-permute-start.4 = (bf16[8,16,16,512]{3,2,1,0:T(8,128)(2,1)}, bf16[8,16,16,512]{3,2,1,0:T(8,128)(2,1)}, u32[]{:S(2)}, u32[]{:S(2)}) collective-permute-start(bf16[8,16,16,512]{3,2,1,0:T(8,128)(2,1)} %all-to-all-done.6), channel_id=1, source_target_pairs={{0,4},{2,6},{4,0},{6,2},{1,5},{3,7},{5,1},{7,3},{8,12},{10,14},{12... | collective-permute-start | bytes 6291464 | tf_op jit(solution)/shard_map/ppermute | solution.py:424
  294.8 137.5 %collective-permute-start.5 = (bf16[8,16,16,512]{3,2,1,0:T(8,128)(2,1)}, bf16[8,16,16,512]{3,2,1,0:T(8,128)(2,1)}, u32[]{:S(2)}, u32[]{:S(2)}) collective-permute-start(bf16[8,16,16,512]{3,2,1,0:T(8,128)(2,1)} %all-to-all-done.7), channel_id=1, source_target_pairs={{0,6},{2,4},{4,2},{6,0},{1,7},{3,5},{5,3},{7,1},{8,14},{10,12},{12... | collective-permute-start | bytes 6291464 | tf_op jit(solution)/shard_map/ppermute | solution.py:424
  303.1 33.7 %all-to-all-start.4 = ((bf16[8,16,16,512]{3,2,1,0:T(8,128)(2,1)}), bf16[8,16,16,512]{3,2,1,0:T(8,128)(2,1)}, u32[]{:S(2)}, u32[]{:S(2)}) async-start(bf16[8,16,16,512]{3,2,1,0:T(8,128)(2,1)} %get-tuple-element.24), calls=%async_computation.4 | async-start | bytes 4194304 | tf_op jit(solution)/shard_map/all_to_all | solution.py:428
  629.0 52.5 %all-to-all-start.13 = ((bf16[8,16,16,512]{3,2,1,0:T(8,128)(2,1)}), bf16[8,16,16,512]{3,2,1,0:T(8,128)(2,1)}, u32[]{:S(2)}, u32[]{:S(2)}) async-start(bf16[8,16,16,512]{3,2,1,0:T(8,128)(2,1)} %bitcast.15), calls=%async_computation.13 | async-start | bytes 4194304 | tf_op jit(solution)/shard_map/all_to_all | solution.py:428
  633.4 136.0 %collective-permute-start.7 = (bf16[8,16,16,512]{3,2,1,0:T(8,128)(2,1)}, bf16[8,16,16,512]{3,2,1,0:T(8,128)(2,1)}, u32[]{:S(2)}, u32[]{:S(2)}) collective-permute-start(bf16[8,16,16,512]{3,2,1,0:T(8,128)(2,1)} %all_to_all.83), channel_id=1, source_target_pairs={{0,2},{2,0},{4,6},{6,4},{1,3},{3,1},{5,7},{7,5},{8,10},{10,8},{12,... | collective-permute-start | bytes 6291464 | tf_op jit(solution)/shard_map/ppermute | solution.py:424
  678.1 229.1 %collective-permute-start.8 = (bf16[8,16,16,512]{3,2,1,0:T(8,128)(2,1)}, bf16[8,16,16,512]{3,2,1,0:T(8,128)(2,1)}, u32[]{:S(2)}, u32[]{:S(2)}) collective-permute-start(bf16[8,16,16,512]{3,2,1,0:T(8,128)(2,1)} %all_to_all.84), channel_id=1, source_target_pairs={{0,4},{2,6},{4,0},{6,2},{1,5},{3,7},{5,1},{7,3},{8,12},{10,14},{12... | collective-permute-start | bytes 6291464 | tf_op jit(solution)/shard_map/ppermute | solution.py:424
  680.1 227.1 %collective-permute-start.9 = (bf16[8,16,16,512]{3,2,1,0:T(8,128)(2,1)}, bf16[8,16,16,512]{3,2,1,0:T(8,128)(2,1)}, u32[]{:S(2)}, u32[]{:S(2)}) collective-permute-start(bf16[8,16,16,512]{3,2,1,0:T(8,128)(2,1)} %all_to_all.85), channel_id=1, source_target_pairs={{0,6},{2,4},{4,2},{6,0},{1,7},{3,5},{5,3},{7,1},{8,14},{10,12},{12... | collective-permute-start | bytes 6291464 | tf_op jit(solution)/shard_map/ppermute | solution.py:424
  681.5 29.9 %all-to-all-start.14 = ((bf16[8,16,16,512]{3,2,1,0:T(8,128)(2,1)}), bf16[8,16,16,512]{3,2,1,0:T(8,128)(2,1)S(1)}, u32[]{:S(2)}, u32[]{:S(2)}) async-start(bf16[8,16,16,512]{3,2,1,0:T(8,128)(2,1)} %bitcast.67), calls=%async_computation.14 | async-start | bytes 4194304 | tf_op jit(solution)/shard_map/all_to_all | solution.py:428
  685.9 326.8 %collective-permute-start.6 = (bf16[8,16,16,512]{3,2,1,0:T(8,128)(2,1)}, bf16[8,16,16,512]{3,2,1,0:T(8,128)(2,1)}, u32[]{:S(2)}, u32[]{:S(2)}) collective-permute-start(bf16[8,16,16,512]{3,2,1,0:T(8,128)(2,1)} %all_to_all.81), channel_id=1, source_target_pairs={{0,6},{2,4},{4,2},{6,0},{1,7},{3,5},{5,3},{7,1},{8,14},{10,12},{12... | collective-permute-start | bytes 6291464 | tf_op jit(solution)/shard_map/ppermute | solution.py:424
  688.3 355.9 %collective-permute-start.10 = (bf16[8,16,16,512]{3,2,1,0:T(8,128)(2,1)}, bf16[8,16,16,512]{3,2,1,0:T(8,128)(2,1)}, u32[]{:S(2)}, u32[]{:S(2)}) collective-permute-start(bf16[8,16,16,512]{3,2,1,0:T(8,128)(2,1)} %all-to-all-done.13), channel_id=1, source_target_pairs={{0,4},{2,6},{4,0},{6,2},{1,5},{3,7},{5,1},{7,3},{8,12},{10,14},{12... | collective-permute-start | bytes 6291464 | tf_op jit(solution)/shard_map/ppermute | solution.py:424
  712.7 339.0 %all-to-all-start.15 = ((bf16[8,16,16,512]{3,2,1,0:T(8,128)(2,1)}), bf16[8,16,16,512]{3,2,1,0:T(8,128)(2,1)S(1)}, u32[]{:S(2)}, u32[]{:S(2)}) async-start(bf16[8,16,16,512]{3,2,1,0:T(8,128)(2,1)} %bitcast.66), calls=%async_computation.15 | async-start | bytes 4194304 | tf_op jit(solution)/shard_map/all_to_all | solution.py:428
  769.4 274.8 %collective-permute-start.11 = (bf16[8,16,16,512]{3,2,1,0:T(8,128)(2,1)}, bf16[8,16,16,512]{3,2,1,0:T(8,128)(2,1)}, u32[]{:S(2)}, u32[]{:S(2)}) collective-permute-start(bf16[8,16,16,512]{3,2,1,0:T(8,128)(2,1)} %copy-done.1), channel_id=1, source_target_pairs={{0,2},{2,0},{4,6},{6,4},{1,3},{3,1},{5,7},{7,5},{8,10},{10,8},{12,... | collective-permute-start | bytes 6291464 | tf_op jit(solution)/shard_map/ppermute | solution.py:424
  942.0 9.9 collective-permute-start.12
  942.0 11.0 %collective-permute-start.13 = (f32[680,128]{1,0:T(8,128)S(1)}, f32[680,128]{1,0:T(8,128)S(1)}, u32[]{:S(2)}, u32[]{:S(2)}) collective-permute-start(f32[680,128]{1,0:T(8,128)S(1)} %get-tuple-element.46), channel_id=1, source_target_pairs={{0,16},{8,24},{16,0},{24,8},{1,17},{9,25},{17,1},{25,9},{2,18},{10... | collective-permute-start | bytes 1044488 | tf_op jit(solution)/shard_map/ppermute | solution.py:437
  951.8 7.3 collective-permute-start.14
  965.2 85.0 %collective-permute-start.15 = (f32[120,128]{1,0:T(8,128)S(1)}, f32[120,128]{1,0:T(8,128)S(1)}, u32[]{:S(2)}, u32[]{:S(2)}) collective-permute-start(f32[120,128]{1,0:T(8,128)S(1)} %get-tuple-element.55), channel_id=1, source_target_pairs={{0,1},{1,2},{2,3},{3,4},{4,5},{5,6},{6,7},{7,0},{8,9},{9,10},{10,1... | collective-permute-start | bytes 184328 | tf_op jit(solution)/shard_map/ppermute | solution.py:437
  966.7 84.8 %collective-permute-start.16 = (f32[120,128]{1,0:T(8,128)S(1)}, f32[120,128]{1,0:T(8,128)S(1)}, u32[]{:S(2)}, u32[]{:S(2)}) collective-permute-start(f32[120,128]{1,0:T(8,128)S(1)} %get-tuple-element.54), channel_id=1, source_target_pairs={{0,2},{1,3},{2,4},{3,5},{4,6},{5,7},{6,0},{7,1},{8,10},{9,11},{10,... | collective-permute-start | bytes 184328 | tf_op jit(solution)/shard_map/ppermute | solution.py:437
  1012.7 57.6 %collective-permute-start.17 = (f32[120,128]{1,0:T(8,128)S(1)}, f32[120,128]{1,0:T(8,128)S(1)}, u32[]{:S(2)}, u32[]{:S(2)}) collective-permute-start(f32[120,128]{1,0:T(8,128)S(1)} %get-tuple-element.53), channel_id=1, source_target_pairs={{0,3},{1,4},{2,5},{3,6},{4,7},{5,0},{6,1},{7,2},{8,11},{9,12},{10,... | collective-permute-start | bytes 184328 | tf_op jit(solution)/shard_map/ppermute | solution.py:437
  1044.2 26.1 %collective-permute-start.18 = (f32[120,128]{1,0:T(8,128)S(1)}, f32[120,128]{1,0:T(8,128)S(1)}, u32[]{:S(2)}, u32[]{:S(2)}) collective-permute-start(f32[120,128]{1,0:T(8,128)S(1)} %get-tuple-element.52), channel_id=1, source_target_pairs={{0,4},{1,5},{2,6},{3,7},{4,0},{5,1},{6,2},{7,3},{8,12},{9,13},{10,... | collective-permute-start | bytes 184328 | tf_op jit(solution)/shard_map/ppermute | solution.py:437
  1044.2 26.1 %collective-permute-start.19 = (f32[120,128]{1,0:T(8,128)S(1)}, f32[120,128]{1,0:T(8,128)S(1)}, u32[]{:S(2)}, u32[]{:S(2)}) collective-permute-start(f32[120,128]{1,0:T(8,128)S(1)} %get-tuple-element.51), channel_id=1, source_target_pairs={{0,5},{1,6},{2,7},{3,0},{4,1},{5,2},{6,3},{7,4},{8,13},{9,14},{10,... | collective-permute-start | bytes 184328 | tf_op jit(solution)/shard_map/ppermute | solution.py:437
  1050.2 20.1 %collective-permute-start.20 = (f32[120,128]{1,0:T(8,128)S(1)}, f32[120,128]{1,0:T(8,128)S(1)}, u32[]{:S(2)}, u32[]{:S(2)}) collective-permute-start(f32[120,128]{1,0:T(8,128)S(1)} %get-tuple-element.50), channel_id=1, source_target_pairs={{0,6},{1,7},{2,0},{3,1},{4,2},{5,3},{6,4},{7,5},{8,14},{9,15},{10,... | collective-permute-start | bytes 184328 | tf_op jit(solution)/shard_map/ppermute | solution.py:437
  1051.5 18.9 %collective-permute-start.21 = (f32[120,128]{1,0:T(8,128)S(1)}, f32[120,128]{1,0:T(8,128)S(1)}, u32[]{:S(2)}, u32[]{:S(2)}) collective-permute-start(f32[120,128]{1,0:T(8,128)S(1)} %get-tuple-element.49), channel_id=1, source_target_pairs={{0,7},{1,0},{2,1},{3,2},{4,3},{5,4},{6,5},{7,6},{8,15},{9,8},{10,9... | collective-permute-start | bytes 184328 | tf_op jit(solution)/shard_map/ppermute | solution.py:437
  (22 other events, 202.5 us)

commit v4 on v3

--- a/solution.py
+++ b/solution.py
@@ -438,22 +438,7 @@
     return out
 
 
-def share_kernel(factor, *refs):
-    total = refs[0][...]
-    for part in refs[1:-1]:
-        total += part[...]
-    refs[-1][...] = total * factor
-
-
-def share_sum(parts, factor):
-    return pl.pallas_call(
-        functools.partial(share_kernel, factor),
-        out_shape=jax.ShapeDtypeStruct(parts[0].shape, F32),
-        name="share_sum",
-    )(*parts)
-
-
-def ordered_kernel(axis, *refs):
+def ordered_kernel(axis, factor, *refs):
     parts, out_ref, held = refs[:-2], refs[-2], refs[-1]
     count = len(parts)
     me = lax.axis_index(axis)
@@ -462,54 +447,58 @@
     total = held[lax.rem(me + count, count)]
     for source in range(1, count):
         total += held[lax.rem(me - source + count, count)]
-    out_ref[...] = total
-
-
-def ordered_sum(parts, axis):
+    out_ref[...] = total * factor
+
+
+def ordered_sum(parts, axis, factor=1.0):
     shape = parts[0].shape
     return pl.pallas_call(
-        functools.partial(ordered_kernel, axis),
+        functools.partial(ordered_kernel, axis, factor),
         out_shape=jax.ShapeDtypeStruct(shape, F32),
         scratch_shapes=[pltpu.VMEM((len(parts),) + shape, F32)],
-        name="ordered_sum",
     )(*parts)
 
 
 def reduced_direct(gate_part, first_part, middle_part, last_part, factor):
-    groups, blocks = lax.axis_size("grp"), lax.axis_size(PLANES)
+    groups, planes, pair_y = (lax.axis_size(axis) for axis in ("grp", "z", "y"))
+    blocks = planes * pair_y
     width = gate_part.shape[0]
     n_last, n_middle, n_first = last_part.shape[1], middle_part.shape[1], first_part.shape[1]
     lane = width // groups
     own = HEADS // groups
 
-    def flat(parts):
-        return parts.reshape(parts.shape[0], -1, lane)
-
+    def both(parts):
+        parts = parts.reshape(groups, 1, -1, lane)
+        return jnp.broadcast_to(parts, (groups, pair_y) + parts.shape[2:])
+
+    gate = gate_part.reshape(planes, pair_y, -1, groups, lane).transpose(3, 1, 0, 2, 4)
+    last = last_part.reshape(groups, own, planes, pair_y, -1).transpose(0, 3, 2, 1, 4)
     packed = jnp.concatenate(
         [
-            gate_part.reshape(width, groups, lane).transpose(1, 0, 2),
-            flat(last_part.reshape(groups, -1)),
-            flat(middle_part.reshape(HEADS, groups, -1).transpose(1, 0, 2)),
-            flat(first_part.reshape(groups, -1)),
+            gate.reshape(groups, pair_y, -1, lane),
+            last.reshape(groups, pair_y, -1, lane),
+            both(middle_part.reshape(HEADS, groups, -1).transpose(1, 0, 2)),
+            both(first_part),
+        ],
+        axis=2,
+    )
+    packed = packed.reshape((groups * pair_y,) + packed.shape[2:])
+    plane = ("grp", "y")
+    mine = lax.dynamic_index_in_dim(packed, lax.axis_index(plane), 0, False)
+    share = ordered_sum([mine] + shifted(packed, plane), plane, factor)
+    cuts = [width // pair_y, own * n_last * n_last // pair_y // lane, HEADS * n_middle * n_middle // groups // lane]
+    gate, last, middle, first = jnp.split(share, [sum(cuts[: n + 1]) for n in range(3)])
+    again = jnp.concatenate(
+        [
+            gate.reshape(planes, -1, lane),
+            last.reshape(planes, -1, lane),
+            jnp.broadcast_to(middle, (planes,) + middle.shape),
+            jnp.broadcast_to(first, (planes,) + first.shape),
         ],
         axis=1,
     )
-    mine = lax.dynamic_index_in_dim(packed, lax.axis_index("grp"), 0, False)
-    share = share_sum([mine] + shifted(packed, "grp"), factor)
-    cuts = [width, own * n_last * n_last // lane, HEADS * n_middle * n_middle // groups // lane]
-    gate, last, middle, first = jnp.split(share, [sum(cuts[: n + 1]) for n in range(3)])
-    last = last.reshape(own, blocks, n_last // blocks, n_last).transpose(1, 0, 2, 3)
-    again = jnp.concatenate(
-        [
-            gate.reshape(blocks, -1, lane),
-            flat(last.reshape(blocks, -1)),
-            jnp.broadcast_to(middle, (blocks,) + middle.shape),
-            jnp.broadcast_to(first, (blocks,) + first.shape),
-        ],
-        axis=1,
-    )
-    mine = lax.dynamic_index_in_dim(again, lax.axis_index(PLANES), 0, False)
-    total = ordered_sum([mine] + shifted(again, PLANES), PLANES)
+    mine = lax.dynamic_index_in_dim(again, lax.axis_index("z"), 0, False)
+    total = ordered_sum([mine] + shifted(again, "z"), "z")
     cuts = [width // blocks, own * n_last * n_last // blocks // lane, middle.shape[0]]
     gate, last, middle, first = jnp.split(total, [sum(cuts[: n + 1]) for n in range(3)])
     give = jnp.concatenate([gate, last, first])
@@ -533,7 +522,10 @@
     split = (groups, pair_y) + tokens.shape[1:]
     home = (part,) + tokens.shape[1:]
     z = lax.axis_index("z")
-    held = [lax.dynamic_slice_in_dim(tokens, (z ^ m) * part, part, 0) for m in range(planes)]
+    held = {}
+    for m in [*range(planes // 2, planes), *range(planes // 2 - 1, -1, -1)]:
+        held[m] = lax.dynamic_slice_in_dim(tokens, (z ^ m) * part, part, 0)
+        z, held[m] = lax.optimization_barrier((z, held[m]))
     at_whole = [in_plane(over_z(held[m], m)).reshape(split) for m in range(planes)]
     sent = open_side(tokens, cotangent, gate_weight, first_factor, planes)
     sent_whole = [over_z(in_plane(sent[m]), m).reshape(split) for m in range(planes)]

time: 1080 us -> 1070 us (level)
  waiting for transfers between devices: 529 us -> 513 us
    ppermute x12, waiting for transfers between devices: 424 us -> 402 us  [over_z(): return lax.ppermute(part, 'z', pairs)]
  transfers between devices with their start and end apart: 35 -> 35, of which waited for: 17 -> 19; matrix products, arithmetic and copies ran while one was open for 1% -> 1% of each run, Pallas kernels for 9% -> 9%
where the time goes in v4:
time: 1070 us
  waiting for transfers between devices  513 us (48%)
  starting transfers between devices  199 us (19%)
  blocking collectives  176 us (16%)
  Pallas kernels  149 us (14%)
  local copies, waits for them, and re-layouts  29.9 us (3%)
    ppermute x12, waiting for transfers between devices, over_z(): return lax.ppermute(part, 'z', pairs)  402 us
    all_to_all x6, blocking collectives, in_plane(): lax.all_to_all(part, ('grp', 'y'), split_axis=0, concat_axis=0, tiled=True)  176 us
    ppermute x12, starting transfers between devices, over_z(): return lax.ppermute(part, 'z', pairs)  96.1 us
    all_to_all x10, waiting for transfers between devices, in_plane(): lax.all_to_all(part, ('grp', 'y'), split_axis=0, concat_axis=0, tiled=True)  89.7 us
    ppermute x13, starting transfers between devices, shifted(): lax.ppermute(part, axis, [(i, (i + d) % count) for i in range(count)])  60.5 us
    pallas_call x1, Pallas kernels, backward_side(): pl.pallas_call(functools.partial(backward_kernel, planes), grid=(HEADS,),...  50.8 us
    all_to_all x10, starting transfers between devices, in_plane(): lax.all_to_all(part, ('grp', 'y'), split_axis=0, concat_axis=0, tiled=True)  42.8 us
    pallas_call x1, Pallas kernels, close_side(): pl.pallas_call(functools.partial(close_kernel, planes, step_j), grid=(n_j...  31.5 us
  transfers between devices with their start and end apart: 35, of which 19 were waited for; matrix products, arithmetic and copies ran while one was open for 1% of the time, Pallas kernels for 9%

profile of v4, /device:TPU:0, one launch (start us, length us, event | category | flops | bytes accessed | tf_op | source)
XLA Modules:
  0.0 1068.4 jit_solution(2789143755747533281)
XLA Ops:
  13.1 5.2 all-to-all-start
  18.3 17.4 %open_side.1 = (bf16[8,16,16,512]{3,2,1,0:T(8,128)(2,1)}, bf16[8,16,16,512]{3,2,1,0:T(8,128)(2,1)}, bf16[8,16,16,512]{3,2,1,0:T(8,128)(2,1)}, bf16[8,16,16,512]{3,2,1,0:T(8,128)(2,1)}) custom-call(bf16[32,16,16,512]{3,2,1,0:T(8,128)(2,1)} %x_ref.3, bf16[32,16,16,512]{3,2,1,0:T(8,128)(2,1)} %g_ref.3, bf16[512,512]{1,0:T(8,128)(2,1)} %w_ref.3, ...), custom_call_target="tpu_custom_call" | custom-call | flops 8589934592 | bytes 25165824 | tf_op jit(solution)/shard_map/open_side/pallas_call | solution.py:169
  35.7 8.4 all-to-all-done
  44.1 30.0 %all_to_all.80 = bf16[8,16,16,512]{3,2,1,0:T(8,128)(2,1)} all-to-all(bf16[8,16,16,512]{3,2,1,0:T(8,128)(2,1)} %get-tuple-element.39), channel_id=1, replica_groups=mesh['grp'=4,'z'=4,'y'=2] {'grp','y'}, dimensions={0} | all-to-all | bytes 4194304 | tf_op jit(solution)/shard_map/all_to_all | solution.py:428
  79.3 24.0 %all-to-all-done.6 = bf16[8,16,16,512]{3,2,1,0:T(8,128)(2,1)S(1)} async-done(((bf16[8,16,16,512]{3,2,1,0:T(8,128)(2,1)}), bf16[8,16,16,512]{3,2,1,0:T(8,128)(2,1)S(1)}, u32[]{:S(2)}, u32[]{:S(2)}) %all-to-all-start.6) | async-done | bytes 2097184 | tf_op jit(solution)/shard_map/all_to_all | solution.py:428
  110.4 23.1 %all-to-all-done.7 = bf16[8,16,16,512]{3,2,1,0:T(8,128)(2,1)} async-done(((bf16[8,16,16,512]{3,2,1,0:T(8,128)(2,1)}), bf16[8,16,16,512]{3,2,1,0:T(8,128)(2,1)}, u32[]{:S(2)}, u32[]{:S(2)}) %all-to-all-start.7) | async-done | bytes 2097184 | tf_op jit(solution)/shard_map/all_to_all | solution.py:428
  133.5 8.6 collective-permute-done
  147.8 99.6 %collective-permute-done.1 = bf16[8,16,16,512]{3,2,1,0:T(8,128)(2,1)} collective-permute-done((bf16[8,16,16,512]{3,2,1,0:T(8,128)(2,1)}, bf16[8,16,16,512]{3,2,1,0:T(8,128)(2,1)}, u32[]{:S(2)}, u32[]{:S(2)}) %collective-permute-start.1) | collective-permute-done | bytes 2097184 | tf_op jit(solution)/shard_map/ppermute | solution.py:424
  247.4 4.4 all-to-all-start.2
  251.8 25.8 %all-to-all-done.2 = bf16[8,16,16,512]{3,2,1,0:T(8,128)(2,1)} async-done(((bf16[8,16,16,512]{3,2,1,0:T(8,128)(2,1)}), bf16[8,16,16,512]{3,2,1,0:T(8,128)(2,1)}, u32[]{:S(2)}, u32[]{:S(2)}) %all-to-all-start.2) | async-done | bytes 2097184 | tf_op jit(solution)/shard_map/all_to_all | solution.py:428
  281.9 15.0 %collective-permute-start.3 = (bf16[8,16,16,512]{3,2,1,0:T(8,128)(2,1)}, bf16[8,16,16,512]{3,2,1,0:T(8,128)(2,1)}, u32[]{:S(2)}, u32[]{:S(2)}) collective-permute-start(bf16[8,16,16,512]{3,2,1,0:T(8,128)(2,1)} %all_to_all.80), channel_id=1, source_target_pairs={{0,2},{2,0},{4,6},{6,4},{1,3},{3,1},{5,7},{7,5},{8,10},{10,8},{12,... | collective-permute-start | bytes 6291464 | tf_op jit(solution)/shard_map/ppermute | solution.py:424
  300.3 7.4 all-to-all-done.3
  307.7 4.5 all-to-all-start.4
  312.9 28.3 %forward_side.1 = (bf16[4,2,16,16,512]{4,3,2,1,0:T(8,128)(2,1)}, bf16[4,2,16,16,512]{4,3,2,1,0:T(8,128)(2,1)}, bf16[4,2,16,16,512]{4,3,2,1,0:T(8,128)(2,1)}, bf1...) custom-call(bf16[4,128,128]{2,1,0:T(8,128)(2,1)} %b_ref.1, bf16[4,64,64]{2,1,0:T(8,128)(2,1)} %c_ref.3, ...), custom_call_target="tpu_custom_call" | custom-call | flops 9663676416 | bytes 25165824 | tf_op jit(solution)/shard_map/forward_side/pallas_call | solution.py:224
  341.2 47.1 %collective-permute-done.3 = bf16[8,16,16,512]{3,2,1,0:T(8,128)(2,1)} collective-permute-done((bf16[8,16,16,512]{3,2,1,0:T(8,128)(2,1)}, bf16[8,16,16,512]{3,2,1,0:T(8,128)(2,1)}, u32[]{:S(2)}, u32[]{:S(2)}) %collective-permute-start.3) | collective-permute-done | bytes 2097184 | tf_op jit(solution)/shard_map/ppermute | solution.py:424
  388.3 48.1 %collective-permute-done.5 = bf16[8,16,16,512]{3,2,1,0:T(8,128)(2,1)} collective-permute-done((bf16[8,16,16,512]{3,2,1,0:T(8,128)(2,1)}, bf16[8,16,16,512]{3,2,1,0:T(8,128)(2,1)}, u32[]{:S(2)}, u32[]{:S(2)}) %collective-permute-start.5) | collective-permute-done | bytes 2097184 | tf_op jit(solution)/shard_map/ppermute | solution.py:424
  436.4 50.8 %backward_side.1 = (bf16[4,2,16,16,512]{4,3,2,1,0:T(8,128)(2,1)}, bf16[4,2,16,16,512]{4,3,2,1,0:T(8,128)(2,1)}, bf16[4,2,16,16,512]{4,3,2,1,0:T(8,128)(2,1)}, bf...) custom-call(bf16[4,128,128]{2,1,0:T(8,128)(2,1)} %bitcast.84, ...), custom_call_target="tpu_custom_call" | custom-call | flops 19327352832 | bytes 33554432 | tf_op jit(solution)/shard_map/backward_side/pallas_call | solution.py:298
  487.2 30.2 %all_to_all.81 = bf16[8,16,16,512]{3,2,1,0:T(8,128)(2,1)} all-to-all(bf16[8,16,16,512]{3,2,1,0:T(8,128)(2,1)} %bitcast.78), channel_id=1, replica_groups=mesh['grp'=4,'z'=4,'y'=2] {'grp','y'}, dimensions={0} | all-to-all | bytes 4194304 | tf_op jit(solution)/shard_map/all_to_all | solution.py:428
  517.4 29.0 %all_to_all.82.refs_0_ = bf16[8,16,16,512]{3,2,1,0:T(8,128)(2,1)} all-to-all(bf16[8,16,16,512]{3,2,1,0:T(8,128)(2,1)S(1)} %bitcast.77), channel_id=1, replica_groups=mesh['grp'=4,'z'=4,'y'=2] {'grp','y'}, dimensions={0} | all-to-all | bytes 4194304 | tf_op jit(solution)/shard_map/all_to_all | solution.py:428
  546.4 29.0 %all_to_all.83 = bf16[8,16,16,512]{3,2,1,0:T(8,128)(2,1)} all-to-all(bf16[8,16,16,512]{3,2,1,0:T(8,128)(2,1)S(1)} %bitcast.76), channel_id=1, replica_groups=mesh['grp'=4,'z'=4,'y'=2] {'grp','y'}, dimensions={0} | all-to-all | bytes 4194304 | tf_op jit(solution)/shard_map/all_to_all | solution.py:428
  575.3 29.0 %all_to_all.84 = bf16[8,16,16,512]{3,2,1,0:T(8,128)(2,1)} all-to-all(bf16[8,16,16,512]{3,2,1,0:T(8,128)(2,1)S(1)} %bitcast.75), channel_id=1, replica_groups=mesh['grp'=4,'z'=4,'y'=2] {'grp','y'}, dimensions={0} | all-to-all | bytes 4194304 | tf_op jit(solution)/shard_map/all_to_all | solution.py:428
  604.3 28.8 %all_to_all.85 = bf16[8,16,16,512]{3,2,1,0:T(8,128)(2,1)} all-to-all(bf16[8,16,16,512]{3,2,1,0:T(8,128)(2,1)S(1)} %bitcast.74), channel_id=1, replica_groups=mesh['grp'=4,'z'=4,'y'=2] {'grp','y'}, dimensions={0} | all-to-all | bytes 4194304 | tf_op jit(solution)/shard_map/all_to_all | solution.py:428
  637.4 44.6 %collective-permute-start.7 = (bf16[8,16,16,512]{3,2,1,0:T(8,128)(2,1)}, bf16[8,16,16,512]{3,2,1,0:T(8,128)(2,1)}, u32[]{:S(2)}, u32[]{:S(2)}) collective-permute-start(bf16[8,16,16,512]{3,2,1,0:T(8,128)(2,1)} %all_to_all.83), channel_id=1, source_target_pairs={{0,2},{2,0},{4,6},{6,4},{1,3},{3,1},{5,7},{7,5},{8,10},{10,8},{12,... | collective-permute-start | bytes 6291464 | tf_op jit(solution)/shard_map/ppermute | solution.py:424
  692.7 21.6 %collective-permute-start.10 = (bf16[8,16,16,512]{3,2,1,0:T(8,128)(2,1)}, bf16[8,16,16,512]{3,2,1,0:T(8,128)(2,1)}, u32[]{:S(2)}, u32[]{:S(2)}) collective-permute-start(bf16[8,16,16,512]{3,2,1,0:T(8,128)(2,1)} %all-to-all-done.13), channel_id=1, source_target_pairs={{0,4},{2,6},{4,0},{6,2},{1,5},{3,7},{5,1},{7,3},{8,12},{10,14},{12... | collective-permute-start | bytes 6291464 | tf_op jit(solution)/shard_map/ppermute | solution.py:424
  720.3 53.1 %collective-permute-done.7.refs_1_ = bf16[8,16,16,512]{3,2,1,0:T(8,128)(2,1)} collective-permute-done((bf16[8,16,16,512]{3,2,1,0:T(8,128)(2,1)}, bf16[8,16,16,512]{3,2,1,0:T(8,128)(2,1)}, u32[]{:S(2)}, u32[]{:S(2)}) %collective-permute-start.7) | collective-permute-done | bytes 2097184 | tf_op jit(solution)/shard_map/ppermute | solution.py:424
  773.3 137.8 %collective-permute-done.8.refs_2_ = bf16[8,16,16,512]{3,2,1,0:T(8,128)(2,1)} collective-permute-done((bf16[8,16,16,512]{3,2,1,0:T(8,128)(2,1)}, bf16[8,16,16,512]{3,2,1,0:T(8,128)(2,1)}, u32[]{:S(2)}, u32[]{:S(2)}) %collective-permute-start.8) | collective-permute-done | bytes 2097184 | tf_op jit(solution)/shard_map/ppermute | solution.py:424
  911.1 31.5 %close_side.1 = (bf16[32,16,16,512]{3,2,1,0:T(8,128)(2,1)}, f32[512,512]{1,0:T(8,128)}, f32[4,32,32]{2,1,0:T(8,128)}) custom-call(bf16[32,16,16,512]{3,2,1,0:T(8,128)(2,1)} %x_ref.3, bf16[32,16,16,512]{3,2,1,0:T(8,128)(2,1)} %g_ref.3, bf16[512,512]{1,0:T(8,128)(2,1)} %w_ref.3, bf16[4,32,32]{2,1,0:T(8,128)(2,1)} %a_ref.3, ...), custom_call_target="tpu_custom_call" | custom-call | flops 21474836480 | bytes 33554432 | tf_op jit(solution)/shard_map/close_side/pallas_call | solution.py:373
  954.4 6.0 collective-permute-done.14.refs_3_
  962.8 4.6 collective-permute-done.16.refs_5_
  968.0 5.3 collective-permute-done.18.refs_7_
  980.1 46.3 %collective-permute-start.19 = (f32[120,128]{1,0:T(8,128)S(1)}, f32[120,128]{1,0:T(8,128)S(1)}, u32[]{:S(2)}, u32[]{:S(2)}) collective-permute-start(f32[120,128]{1,0:T(8,128)S(1)} %get-tuple-element.65), channel_id=1, source_target_pairs={{0,2},{2,4},{4,6},{6,0},{1,3},{3,5},{5,7},{7,1},{8,10},{10,12},{12... | collective-permute-start | bytes 184328 | tf_op jit(solution)/shard_map/ppermute | solution.py:437
  1041.1 7.9 collective-permute-done.10.b_ref
  (134 shorter events, 115.3 us)
Async XLA Ops:
  13.1 31.0 %all-to-all-start = ((bf16[8,16,16,512]{3,2,1,0:T(8,128)(2,1)}), bf16[8,16,16,512]{3,2,1,0:T(8,128)(2,1)S(1)}, u32[]{:S(2)}, u32[]{:S(2)}) async-start(bf16[8,16,16,512]{3,2,1,0:T(8,128)(2,1)} %constant_dynamic-slice_fusion), calls=%async_computation | async-start | bytes 4194304 | tf_op jit(solution)/shard_map/all_to_all | solution.py:428
  74.1 29.3 %all-to-all-start.6 = ((bf16[8,16,16,512]{3,2,1,0:T(8,128)(2,1)}), bf16[8,16,16,512]{3,2,1,0:T(8,128)(2,1)S(1)}, u32[]{:S(2)}, u32[]{:S(2)}) async-start(bf16[8,16,16,512]{3,2,1,0:T(8,128)(2,1)} %get-tuple-element.40), calls=%async_computation.6 | async-start | bytes 4194304 | tf_op jit(solution)/shard_map/all_to_all | solution.py:428
  77.7 64.4 %collective-permute-start = (bf16[8,16,16,512]{3,2,1,0:T(8,128)(2,1)}, bf16[8,16,16,512]{3,2,1,0:T(8,128)(2,1)}, u32[]{:S(2)}, u32[]{:S(2)}) collective-permute-start(bf16[8,16,16,512]{3,2,1,0:T(8,128)(2,1)} %constant_dynamic-slice_fusion.1), channel_id=1, source_target_pairs={{0,2},{2,0},{4,6},{6,4},{1,3},{3,1},{5,7},{7,5},{8,10},{10,8},{12,... | collective-permute-start | bytes 6291464 | tf_op jit(solution)/shard_map/ppermute | solution.py:424
  103.4 30.1 %all-to-all-start.7 = ((bf16[8,16,16,512]{3,2,1,0:T(8,128)(2,1)}), bf16[8,16,16,512]{3,2,1,0:T(8,128)(2,1)}, u32[]{:S(2)}, u32[]{:S(2)}) async-start(bf16[8,16,16,512]{3,2,1,0:T(8,128)(2,1)} %get-tuple-element.41), calls=%async_computation.7 | async-start | bytes 4194304 | tf_op jit(solution)/shard_map/all_to_all | solution.py:428
  107.7 139.7 %collective-permute-start.1 = (bf16[8,16,16,512]{3,2,1,0:T(8,128)(2,1)}, bf16[8,16,16,512]{3,2,1,0:T(8,128)(2,1)}, u32[]{:S(2)}, u32[]{:S(2)}) collective-permute-start(bf16[8,16,16,512]{3,2,1,0:T(8,128)(2,1)} %constant_dynamic-slice_fusion.3), channel_id=1, source_target_pairs={{0,4},{2,6},{4,0},{6,2},{1,5},{3,7},{5,1},{7,3},{8,12},{10,14},{12... | collective-permute-start | bytes 6291464 | tf_op jit(solution)/shard_map/ppermute | solution.py:424
  142.1 105.4 %all-to-all-start.1 = ((bf16[8,16,16,512]{3,2,1,0:T(8,128)(2,1)}), bf16[8,16,16,512]{3,2,1,0:T(8,128)(2,1)}, u32[]{:S(2)}, u32[]{:S(2)}) async-start(bf16[8,16,16,512]{3,2,1,0:T(8,128)(2,1)} %collective-permute-done), calls=%async_computation.1 | async-start | bytes 4194304 | tf_op jit(solution)/shard_map/all_to_all | solution.py:428
  146.4 105.4 %collective-permute-start.2 = (bf16[8,16,16,512]{3,2,1,0:T(8,128)(2,1)}, bf16[8,16,16,512]{3,2,1,0:T(8,128)(2,1)}, u32[]{:S(2)}, u32[]{:S(2)}) collective-permute-start(bf16[8,16,16,512]{3,2,1,0:T(8,128)(2,1)} %constant_dynamic-slice_fusion.2), channel_id=1, source_target_pairs={{0,6},{2,4},{4,2},{6,0},{1,7},{3,5},{5,3},{7,1},{8,14},{10,12},{12... | collective-permute-start | bytes 6291464 | tf_op jit(solution)/shard_map/ppermute | solution.py:424
  247.4 30.1 %all-to-all-start.2 = ((bf16[8,16,16,512]{3,2,1,0:T(8,128)(2,1)}), bf16[8,16,16,512]{3,2,1,0:T(8,128)(2,1)}, u32[]{:S(2)}, u32[]{:S(2)}) async-start(bf16[8,16,16,512]{3,2,1,0:T(8,128)(2,1)} %collective-permute-done.1), calls=%async_computation.2 | async-start | bytes 4194304 | tf_op jit(solution)/shard_map/all_to_all | solution.py:428
  277.5 30.1 %all-to-all-start.3 = ((bf16[8,16,16,512]{3,2,1,0:T(8,128)(2,1)}), bf16[8,16,16,512]{3,2,1,0:T(8,128)(2,1)}, u32[]{:S(2)}, u32[]{:S(2)}) async-start(bf16[8,16,16,512]{3,2,1,0:T(8,128)(2,1)} %collective-permute-done.2), calls=%async_computation.3 | async-start | bytes 4194304 | tf_op jit(solution)/shard_map/all_to_all | solution.py:428
  281.9 106.4 %collective-permute-start.3 = (bf16[8,16,16,512]{3,2,1,0:T(8,128)(2,1)}, bf16[8,16,16,512]{3,2,1,0:T(8,128)(2,1)}, u32[]{:S(2)}, u32[]{:S(2)}) collective-permute-start(bf16[8,16,16,512]{3,2,1,0:T(8,128)(2,1)} %all_to_all.80), channel_id=1, source_target_pairs={{0,2},{2,0},{4,6},{6,4},{1,3},{3,1},{5,7},{7,5},{8,10},{10,8},{12,... | collective-permute-start | bytes 6291464 | tf_op jit(solution)/shard_map/ppermute | solution.py:424
  296.9 91.4 %collective-permute-start.4 = (bf16[8,16,16,512]{3,2,1,0:T(8,128)(2,1)S(1)}, bf16[8,16,16,512]{3,2,1,0:T(8,128)(2,1)}, u32[]{:S(2)}, u32[]{:S(2)}) collective-permute-start(bf16[8,16,16,512]{3,2,1,0:T(8,128)(2,1)S(1)} %all-to-all-done.6), channel_id=1, source_target_pairs={{0,4},{2,6},{4,0},{6,2},{1,5},{3,7},{5,1},{7,3},{8,12},{10,14},{12... | collective-permute-start | bytes 6291464 | tf_op jit(solution)/shard_map/ppermute | solution.py:424
  298.9 137.5 %collective-permute-start.5 = (bf16[8,16,16,512]{3,2,1,0:T(8,128)(2,1)}, bf16[8,16,16,512]{3,2,1,0:T(8,128)(2,1)}, u32[]{:S(2)}, u32[]{:S(2)}) collective-permute-start(bf16[8,16,16,512]{3,2,1,0:T(8,128)(2,1)} %all-to-all-done.7), channel_id=1, source_target_pairs={{0,6},{2,4},{4,2},{6,0},{1,7},{3,5},{5,3},{7,1},{8,14},{10,12},{12... | collective-permute-start | bytes 6291464 | tf_op jit(solution)/shard_map/ppermute | solution.py:424
  307.7 33.5 %all-to-all-start.4 = ((bf16[8,16,16,512]{3,2,1,0:T(8,128)(2,1)}), bf16[8,16,16,512]{3,2,1,0:T(8,128)(2,1)}, u32[]{:S(2)}, u32[]{:S(2)}) async-start(bf16[8,16,16,512]{3,2,1,0:T(8,128)(2,1)} %get-tuple-element.38), calls=%async_computation.4 | async-start | bytes 4194304 | tf_op jit(solution)/shard_map/all_to_all | solution.py:428
  633.1 52.3 %all-to-all-start.13 = ((bf16[8,16,16,512]{3,2,1,0:T(8,128)(2,1)}), bf16[8,16,16,512]{3,2,1,0:T(8,128)(2,1)}, u32[]{:S(2)}, u32[]{:S(2)}) async-start(bf16[8,16,16,512]{3,2,1,0:T(8,128)(2,1)} %bitcast.15), calls=%async_computation.13 | async-start | bytes 4194304 | tf_op jit(solution)/shard_map/all_to_all | solution.py:428
  637.4 135.9 %collective-permute-start.7 = (bf16[8,16,16,512]{3,2,1,0:T(8,128)(2,1)}, bf16[8,16,16,512]{3,2,1,0:T(8,128)(2,1)}, u32[]{:S(2)}, u32[]{:S(2)}) collective-permute-start(bf16[8,16,16,512]{3,2,1,0:T(8,128)(2,1)} %all_to_all.83), channel_id=1, source_target_pairs={{0,2},{2,0},{4,6},{6,4},{1,3},{3,1},{5,7},{7,5},{8,10},{10,8},{12,... | collective-permute-start | bytes 6291464 | tf_op jit(solution)/shard_map/ppermute | solution.py:424
  682.0 229.1 %collective-permute-start.8 = (bf16[8,16,16,512]{3,2,1,0:T(8,128)(2,1)}, bf16[8,16,16,512]{3,2,1,0:T(8,128)(2,1)}, u32[]{:S(2)}, u32[]{:S(2)}) collective-permute-start(bf16[8,16,16,512]{3,2,1,0:T(8,128)(2,1)} %all_to_all.84), channel_id=1, source_target_pairs={{0,4},{2,6},{4,0},{6,2},{1,5},{3,7},{5,1},{7,3},{8,12},{10,14},{12... | collective-permute-start | bytes 6291464 | tf_op jit(solution)/shard_map/ppermute | solution.py:424
  684.0 227.1 %collective-permute-start.9 = (bf16[8,16,16,512]{3,2,1,0:T(8,128)(2,1)}, bf16[8,16,16,512]{3,2,1,0:T(8,128)(2,1)}, u32[]{:S(2)}, u32[]{:S(2)}) collective-permute-start(bf16[8,16,16,512]{3,2,1,0:T(8,128)(2,1)} %all_to_all.85), channel_id=1, source_target_pairs={{0,6},{2,4},{4,2},{6,0},{1,7},{3,5},{5,3},{7,1},{8,14},{10,12},{12... | collective-permute-start | bytes 6291464 | tf_op jit(solution)/shard_map/ppermute | solution.py:424
  685.4 29.9 %all-to-all-start.14 = ((bf16[8,16,16,512]{3,2,1,0:T(8,128)(2,1)}), bf16[8,16,16,512]{3,2,1,0:T(8,128)(2,1)S(1)}, u32[]{:S(2)}, u32[]{:S(2)}) async-start(bf16[8,16,16,512]{3,2,1,0:T(8,128)(2,1)} %bitcast.71), calls=%async_computation.14 | async-start | bytes 4194304 | tf_op jit(solution)/shard_map/all_to_all | solution.py:428
  690.3 363.1 %collective-permute-start.6 = (bf16[8,16,16,512]{3,2,1,0:T(8,128)(2,1)}, bf16[8,16,16,512]{3,2,1,0:T(8,128)(2,1)}, u32[]{:S(2)}, u32[]{:S(2)}) collective-permute-start(bf16[8,16,16,512]{3,2,1,0:T(8,128)(2,1)} %all_to_all.81), channel_id=1, source_target_pairs={{0,6},{2,4},{4,2},{6,0},{1,7},{3,5},{5,3},{7,1},{8,14},{10,12},{12... | collective-permute-start | bytes 6291464 | tf_op jit(solution)/shard_map/ppermute | solution.py:424
  692.7 356.4 %collective-permute-start.10 = (bf16[8,16,16,512]{3,2,1,0:T(8,128)(2,1)}, bf16[8,16,16,512]{3,2,1,0:T(8,128)(2,1)}, u32[]{:S(2)}, u32[]{:S(2)}) collective-permute-start(bf16[8,16,16,512]{3,2,1,0:T(8,128)(2,1)} %all-to-all-done.13), channel_id=1, source_target_pairs={{0,4},{2,6},{4,0},{6,2},{1,5},{3,7},{5,1},{7,3},{8,12},{10,14},{12... | collective-permute-start | bytes 6291464 | tf_op jit(solution)/shard_map/ppermute | solution.py:424
  716.6 314.6 %all-to-all-start.15 = ((bf16[8,16,16,512]{3,2,1,0:T(8,128)(2,1)}), bf16[8,16,16,512]{3,2,1,0:T(8,128)(2,1)S(1)}, u32[]{:S(2)}, u32[]{:S(2)}) async-start(bf16[8,16,16,512]{3,2,1,0:T(8,128)(2,1)} %bitcast.70), calls=%async_computation.15 | async-start | bytes 4194304 | tf_op jit(solution)/shard_map/all_to_all | solution.py:428
  773.3 255.0 %collective-permute-start.11 = (bf16[8,16,16,512]{3,2,1,0:T(8,128)(2,1)}, bf16[8,16,16,512]{3,2,1,0:T(8,128)(2,1)}, u32[]{:S(2)}, u32[]{:S(2)}) collective-permute-start(bf16[8,16,16,512]{3,2,1,0:T(8,128)(2,1)} %copy-done.1), channel_id=1, source_target_pairs={{0,2},{2,0},{4,6},{6,4},{1,3},{3,1},{5,7},{7,5},{8,10},{10,8},{12,... | collective-permute-start | bytes 6291464 | tf_op jit(solution)/shard_map/ppermute | solution.py:424
  946.2 6.0 collective-permute-start.12
  948.0 5.0 collective-permute-start.13
  952.2 8.3 collective-permute-start.14
  953.0 8.8 collective-permute-start.15
  960.5 6.9 collective-permute-start.16
  961.7 6.3 collective-permute-start.17
  967.4 5.9 collective-permute-start.18
  980.1 77.6 %collective-permute-start.19 = (f32[120,128]{1,0:T(8,128)S(1)}, f32[120,128]{1,0:T(8,128)S(1)}, u32[]{:S(2)}, u32[]{:S(2)}) collective-permute-start(f32[120,128]{1,0:T(8,128)S(1)} %get-tuple-element.65), channel_id=1, source_target_pairs={{0,2},{2,4},{4,6},{6,0},{1,3},{3,5},{5,7},{7,1},{8,10},{10,12},{12... | collective-permute-start | bytes 184328 | tf_op jit(solution)/shard_map/ppermute | solution.py:437
  1026.4 31.3 %collective-permute-start.20 = (f32[120,128]{1,0:T(8,128)S(1)}, f32[120,128]{1,0:T(8,128)S(1)}, u32[]{:S(2)}, u32[]{:S(2)}) collective-permute-start(f32[120,128]{1,0:T(8,128)S(1)} %get-tuple-element.64), channel_id=1, source_target_pairs={{0,4},{2,6},{4,0},{6,2},{1,5},{3,7},{5,1},{7,3},{8,12},{10,14},{12... | collective-permute-start | bytes 184328 | tf_op jit(solution)/shard_map/ppermute | solution.py:437
  1028.3 29.4 %collective-permute-start.21 = (f32[120,128]{1,0:T(8,128)S(1)}, f32[120,128]{1,0:T(8,128)S(1)}, u32[]{:S(2)}, u32[]{:S(2)}) collective-permute-start(f32[120,128]{1,0:T(8,128)S(1)} %get-tuple-element.63), channel_id=1, source_target_pairs={{0,6},{2,0},{4,2},{6,4},{1,7},{3,1},{5,3},{7,5},{8,14},{10,8},{12,... | collective-permute-start | bytes 184328 | tf_op jit(solution)/shard_map/ppermute | solution.py:437
  (23 other events, 255.1 us)
